TPU v7x, 32 devices: a whole 2x2x4 slice. The times are simulated.
32 devices in a mesh: dp: 8 (over z, x), tensor: 4 (over y, core).
Axes of the slice: x: 2, y: 2, z: 4, core: 2. Of those that a mesh axis runs over, the one named last changes fastest.
Arguments:
- tokens: bfloat16 [32768, 768], P(('dp', 'tensor')), may hold values from -6 to 6
- cotangent: bfloat16 [32768, 768], P(('dp', 'tensor')), may hold values from -6 to 6
- tie_index: int32 [1], replicated, may hold values from 0 to 11
- image_start: int32 [8], P('dp'), may hold values from 0 to 3840
- qkv_bank: bfloat16 [12, 768, 3, 768], P(None, 'dp', None, 'tensor'), may hold values from -0.21875 to 0.21875
- out_bank: bfloat16 [12, 768, 768], P(None, 'tensor', 'dp'), may hold values from -3.5 to 3.5
- up_bank: bfloat16 [12, 768, 3072], P(None, 'dp', 'tensor'), may hold values from -0.21875 to 0.21875
- down_bank: bfloat16 [12, 3072, 768], P(None, 'tensor', 'dp'), may hold values from -0.109375 to 0.109375
- gain_bank: bfloat16 [12, 2, 768], P(None, None, 'dp'), may hold values from 0.25 to 1.75
- shift_bank: bfloat16 [12, 4, 768], P(None, None, 'dp'), may hold values from -1.5 to 1.5
- head_bias_bank: bfloat16 [12, 2, 768], P(None, None, ('tensor', 'dp')), may hold values from -1.5 to 1.5
- hidden_bias_bank: bfloat16 [12, 3072], P(None, ('tensor', 'dp')), may hold values from -1.5 to 1.5
Outputs:
- layer_out: bfloat16 [32768, 768], P(('dp', 'tensor'))
- grad_tokens: bfloat16 [32768, 768], P(('dp', 'tensor'))
- grad_qkv: float32 [768, 3, 768], P('dp', None, 'tensor')
- grad_out: float32 [768, 768], P('tensor', 'dp')
- grad_up: float32 [768, 3072], P('dp', 'tensor')
- grad_down: float32 [3072, 768], P('tensor', 'dp')
- grad_gains: float32 [2, 768], P(None, 'dp')
- grad_shifts: float32 [4, 768], P(None, 'dp')
- grad_head_bias: float32 [2, 768], P(None, ('tensor', 'dp'))
- grad_hidden_bias: float32 [3072], P(('tensor', 'dp'))
Inputs may be any that keep to these rules, and one draw needn't show every extreme that they name: `tie_index`: which of the 12 weight sets the block uses. Each sequence's image span is positions image_start to image_start + 255.
All inputs are finite; a program needn't handle non-finite values.
Results may differ from a plain program's by a relative error of at most 0.017.
Values may be sent and summed in bfloat16 or wider, within the bound.
No kernel may reach another device: no remote copies, remote signals or barrier semaphores. Data moves between devices by JAX's collectives and lax.ppermute only.
A program may use at most 256 MiB of HBM per device.

v0:
```python
import math

import jax
import jax.numpy as jnp
from jax import lax
from jax.sharding import PartitionSpec as P

HEAD_DIM = 64
SEQ_LEN = 4096
IMG = 256


EPSILON = 1e-05


def norm_rows(values, gain, shift):
    average = jnp.mean(values, axis=-1, keepdims=True)
    centred = values - average
    spread = jnp.mean(centred * centred, axis=-1, keepdims=True)
    return centred * lax.rsqrt(spread + EPSILON) * gain + shift


def gelu_tanh(values):
    inner_arg = 0.7978845608028654 * (values + 0.044715 * values * values * values)
    return 0.5 * values * (1.0 + jnp.tanh(inner_arg))


def visible_mask(query_pos, key_pos, span_first):
    causal = key_pos[None, :] <= query_pos[:, None]
    query_in = (query_pos >= span_first) & (query_pos < span_first + IMG)
    key_in = (key_pos >= span_first) & (key_pos < span_first + IMG)
    return causal | query_in[:, None] & key_in[None, :]


def attend_forward(queries, keys_low, values, starts, block_rows):
    sequences, length, head_count, head_width = queries.shape
    block_count = length // block_rows
    factor = 1.0 / math.sqrt(head_width)
    key_pos = jnp.arange(length, dtype=jnp.int32)

    def one_sequence(element):
        query_seq, key_seq, value_seq, span_first = element
        query_blocks = query_seq.reshape(block_count, block_rows, head_count, head_width)

        def one_block(argument):
            query_block, position = argument
            query_pos = position * block_rows + jnp.arange(block_rows, dtype=jnp.int32)
            scores = (
                jnp.einsum("qhe,khe->hqk", query_block, key_seq, preferred_element_type=jnp.float32)
                * factor
            )
            visible = visible_mask(query_pos, key_pos, span_first)
            scores = jnp.where(visible[None], scores, -1e30)
            highest = jnp.max(scores, axis=-1, keepdims=True)
            raised = jnp.exp(scores - highest)
            summed = jnp.sum(raised, axis=-1, keepdims=True)
            weights = (raised / summed).astype(jnp.bfloat16)
            mixed_out = jnp.einsum(
                "hqk,khe->qhe", weights, value_seq, preferred_element_type=jnp.float32
            )
            return (mixed_out.astype(jnp.bfloat16), (highest + jnp.log(summed))[..., 0])

        return lax.map(one_block, (query_blocks, jnp.arange(block_count, dtype=jnp.int32)))

    mixed_out, log_totals = lax.map(one_sequence, (queries, keys_low, values, starts))
    return (mixed_out.reshape(sequences * length, head_count * head_width), log_totals)


def attend_backward(queries, keys_low, values, starts, log_totals, grad_mixed, block_rows):
    sequences, length, head_count, head_width = queries.shape
    block_count = length // block_rows
    factor = 1.0 / math.sqrt(head_width)
    key_pos = jnp.arange(length, dtype=jnp.int32)

    def one_sequence(element):
        query_seq, key_seq, value_seq, span_first, log_seq, grad_seq = element
        query_blocks = query_seq.reshape(block_count, block_rows, head_count, head_width)
        grad_blocks = grad_seq.reshape(block_count, block_rows, head_count, head_width)

        def one_block(running, argument):
            grad_keys, grad_values = running
            query_block, grad_block, log_block, position = argument
            query_pos = position * block_rows + jnp.arange(block_rows, dtype=jnp.int32)
            scores = (
                jnp.einsum("qhe,khe->hqk", query_block, key_seq, preferred_element_type=jnp.float32)
                * factor
            )
            visible = visible_mask(query_pos, key_pos, span_first)
            weights = jnp.where(visible[None], jnp.exp(scores - log_block[..., None]), 0.0)
            grad_weights = jnp.einsum(
                "qhe,khe->hqk", grad_block, value_seq, preferred_element_type=jnp.float32
            )
            centre = jnp.sum(grad_weights * weights, axis=-1, keepdims=True)
            grad_scores = (weights * (grad_weights - centre)).astype(jnp.bfloat16)
            grad_values = grad_values + jnp.einsum(
                "hqk,qhe->khe",
                weights.astype(jnp.bfloat16),
                grad_block,
                preferred_element_type=jnp.float32,
            )
            grad_keys = grad_keys + factor * jnp.einsum(
                "hqk,qhe->khe", grad_scores, query_block, preferred_element_type=jnp.float32
            )
            grad_query = factor * jnp.einsum(
                "hqk,khe->qhe", grad_scores, key_seq, preferred_element_type=jnp.float32
            )
            return ((grad_keys, grad_values), grad_query)

        zero_heads = jnp.zeros((length, head_count, head_width), jnp.float32)
        (grad_keys, grad_values), grad_query = lax.scan(
            one_block,
            (zero_heads, zero_heads),
            (query_blocks, grad_blocks, log_seq, jnp.arange(block_count, dtype=jnp.int32)),
        )
        return (grad_query.reshape(length, head_count, head_width), grad_keys, grad_values)

    grad_query, grad_keys, grad_values = lax.map(
        one_sequence, (queries, keys_low, values, starts, log_totals, grad_mixed)
    )
    flat = (sequences * length, head_count * head_width)
    return (grad_query.reshape(flat), grad_keys.reshape(flat), grad_values.reshape(flat))


def local(
    tokens,
    cotangent,
    tie_index,
    image_start,
    qkv_bank,
    out_bank,
    up_bank,
    down_bank,
    gain_bank,
    shift_bank,
    head_bias_bank,
    hidden_bias_bank,
):
    chosen = tie_index[0]
    qkv_part = lax.dynamic_index_in_dim(qkv_bank, chosen, 0, keepdims=False)
    out_part = lax.dynamic_index_in_dim(out_bank, chosen, 0, keepdims=False)
    up_part = lax.dynamic_index_in_dim(up_bank, chosen, 0, keepdims=False)
    down_part = lax.dynamic_index_in_dim(down_bank, chosen, 0, keepdims=False)
    gain_part = lax.dynamic_index_in_dim(gain_bank, chosen, 0, keepdims=False)
    shift_part = lax.dynamic_index_in_dim(shift_bank, chosen, 0, keepdims=False)
    head_part = lax.dynamic_index_in_dim(head_bias_bank, chosen, 0, keepdims=False)
    hidden_part = lax.dynamic_index_in_dim(hidden_bias_bank, chosen, 0, keepdims=False)
    w_qkv, w_out, w_up, w_down, gains, shifts, head_bias, hidden_bias = (
        lax.all_gather(qkv_part, "dp", axis=0, tiled=True),
        lax.all_gather(out_part, "dp", axis=1, tiled=True),
        lax.all_gather(up_part, "dp", axis=0, tiled=True),
        lax.all_gather(down_part, "dp", axis=1, tiled=True),
        lax.all_gather(gain_part, "dp", axis=1, tiled=True),
        lax.all_gather(shift_part, "dp", axis=1, tiled=True),
        lax.all_gather(head_part, "dp", axis=1, tiled=True),
        lax.all_gather(hidden_part, "dp", axis=0, tiled=True),
    )
    sequences = image_start.shape[0]
    block_rows = min(512, SEQ_LEN)
    local_width = w_qkv.shape[2]
    local_heads = local_width // HEAD_DIM
    gains_wide = gains.astype(jnp.float32)
    shifts_wide = shifts.astype(jnp.float32)
    head_wide = head_bias.astype(jnp.float32)
    inputs = tokens.astype(jnp.float32)
    normed_one = norm_rows(inputs, gains_wide[0], shifts_wide[0]).astype(jnp.bfloat16)
    rows_one = lax.all_gather(normed_one, "tensor", axis=0, tiled=True)
    projected = jnp.einsum("td,dce->tce", rows_one, w_qkv, preferred_element_type=jnp.float32)
    queries = (projected[:, 0] + head_wide[0]).astype(jnp.bfloat16)
    keys_low = projected[:, 1].astype(jnp.bfloat16)
    values = (projected[:, 2] + head_wide[1]).astype(jnp.bfloat16)
    shaped = (sequences, SEQ_LEN, local_heads, HEAD_DIM)
    query_heads = queries.reshape(shaped)
    key_heads = keys_low.reshape(shaped)
    value_heads = values.reshape(shaped)
    mixed_out, log_totals = attend_forward(
        query_heads, key_heads, value_heads, image_start, block_rows
    )
    portion = mixed_out
    attended = lax.psum_scatter(
        jnp.dot(portion, w_out, preferred_element_type=jnp.float32).astype(jnp.bfloat16),
        "tensor",
        scatter_dimension=0,
        tiled=True,
    ).astype(jnp.float32)
    middle = inputs + attended + shifts_wide[2]
    normed_two = norm_rows(middle, gains_wide[1], shifts_wide[1]).astype(jnp.bfloat16)
    grad_result = cotangent.astype(jnp.float32)
    rows_two = lax.all_gather(normed_two, "tensor", axis=0, tiled=True)
    pre_act = jnp.dot(rows_two, w_up, preferred_element_type=jnp.float32) + hidden_bias.astype(
        jnp.float32
    )
    activ = gelu_tanh(pre_act).astype(jnp.bfloat16)
    portion = activ
    branch = lax.psum_scatter(
        jnp.dot(portion, w_down, preferred_element_type=jnp.float32).astype(jnp.bfloat16),
        "tensor",
        scatter_dimension=0,
        tiled=True,
    ).astype(jnp.float32)
    portion = lax.all_gather(cotangent, "tensor", axis=0, tiled=True)
    grad_down_acc = jnp.einsum("tf,td->fd", activ, portion, preferred_element_type=jnp.float32)
    grad_rows = jnp.einsum("td,fd->tf", portion, w_down, preferred_element_type=jnp.float32)
    grad_act_acc = grad_rows
    grad_pre = jax.vjp(gelu_tanh, pre_act)[1](grad_act_acc)[0].astype(jnp.bfloat16)
    grad_up = jnp.einsum("td,tf->df", rows_two, grad_pre, preferred_element_type=jnp.float32)
    grad_hidden = jnp.sum(grad_pre, axis=0, dtype=jnp.float32)
    portion = grad_pre
    grad_normed_two = lax.psum_scatter(
        jnp.einsum("tf,df->td", portion, w_up, preferred_element_type=jnp.float32).astype(
            jnp.bfloat16
        ),
        "tensor",
        scatter_dimension=0,
        tiled=True,
    ).astype(jnp.float32)
    result = middle + branch + shifts_wide[3]
    pull_two = jax.vjp(norm_rows, middle, gains_wide[1], shifts_wide[1])[1]
    grad_middle_norm, grad_gain_two, grad_shift_two = pull_two(grad_normed_two)
    grad_middle = grad_result + grad_middle_norm
    grad_attended = grad_middle.astype(jnp.bfloat16)
    grad_attn_bias = jnp.sum(grad_attended, axis=0, dtype=jnp.float32)
    portion = lax.all_gather(grad_attended, "tensor", axis=0, tiled=True)
    grad_out_acc = jnp.einsum("te,td->ed", mixed_out, portion, preferred_element_type=jnp.float32)
    grad_rows = jnp.einsum("td,ed->te", portion, w_out, preferred_element_type=jnp.float32)
    grad_mixed_low = grad_rows.astype(jnp.bfloat16).reshape(shaped)
    grad_query, grad_keys, grad_values = attend_backward(
        query_heads, key_heads, value_heads, image_start, log_totals, grad_mixed_low, block_rows
    )
    grad_query = grad_query.astype(jnp.bfloat16)
    grad_keys = grad_keys.astype(jnp.bfloat16)
    grad_values = grad_values.astype(jnp.bfloat16)
    grad_proj = jnp.stack([grad_query, grad_keys, grad_values], axis=1)
    grad_qkv = jnp.einsum("td,tce->dce", rows_one, grad_proj, preferred_element_type=jnp.float32)
    grad_head = jnp.stack(
        [
            jnp.sum(grad_query, axis=0, dtype=jnp.float32),
            jnp.sum(grad_values, axis=0, dtype=jnp.float32),
        ]
    )
    portion = grad_proj
    grad_normed_one = lax.psum_scatter(
        jnp.einsum("tce,dce->td", portion, w_qkv, preferred_element_type=jnp.float32).astype(
            jnp.bfloat16
        ),
        "tensor",
        scatter_dimension=0,
        tiled=True,
    ).astype(jnp.float32)
    pull_one = jax.vjp(norm_rows, inputs, gains_wide[0], shifts_wide[0])[1]
    grad_input_norm, grad_gain_one, grad_shift_one = pull_one(grad_normed_one)
    grad_tokens = (grad_middle + grad_input_norm).astype(jnp.bfloat16)
    gains_local = jnp.stack([grad_gain_one, grad_gain_two])
    shifts_local = jnp.stack(
        [grad_shift_one, grad_shift_two, grad_attn_bias, jnp.sum(grad_result, axis=0)]
    )
    (
        qkv_shard,
        out_shard,
        up_shard,
        down_shard,
        gain_shard,
        shift_shard,
        head_shard,
        hidden_shard,
    ) = (
        lax.psum_scatter(grad_qkv, "dp", scatter_dimension=0, tiled=True),
        lax.psum_scatter(grad_out_acc, "dp", scatter_dimension=1, tiled=True),
        lax.psum_scatter(grad_up, "dp", scatter_dimension=0, tiled=True),
        lax.psum_scatter(grad_down_acc, "dp", scatter_dimension=1, tiled=True),
        lax.psum_scatter(gains_local, "dp", scatter_dimension=1, tiled=True),
        lax.psum_scatter(shifts_local, "dp", scatter_dimension=1, tiled=True),
        lax.psum_scatter(grad_head, "dp", scatter_dimension=1, tiled=True),
        lax.psum_scatter(grad_hidden, "dp", scatter_dimension=0, tiled=True),
    )
    gain_total, shift_total = lax.psum((gain_shard, shift_shard), "tensor")
    return (
        result.astype(jnp.bfloat16),
        grad_tokens,
        qkv_shard,
        out_shard,
        up_shard,
        down_shard,
        gain_total,
        shift_total,
        head_shard,
        hidden_shard,
    )


def solution(mesh):
    placed = (
        P(("dp", "tensor"), None),
        P(("dp", "tensor"), None),
        P(),
        P("dp"),
        P(None, "dp", None, "tensor"),
        P(None, "tensor", "dp"),
        P(None, "dp", "tensor"),
        P(None, "tensor", "dp"),
        P(None, None, "dp"),
        P(None, None, "dp"),
        P(None, None, ("tensor", "dp")),
        P(None, ("tensor", "dp")),
    )
    return jax.shard_map(
        local,
        mesh=mesh,
        in_specs=placed,
        out_specs=(
            P(("dp", "tensor"), None),
            P(("dp", "tensor"), None),
            P("dp", None, "tensor"),
            P("tensor", "dp"),
            P("dp", "tensor"),
            P("tensor", "dp"),
            P(None, "dp"),
            P(None, "dp"),
            P(None, ("tensor", "dp")),
            P(("tensor", "dp")),
        ),
        check_vma=False,
    )
```

profile of v0, /device:TPU:0, one launch (start us, length us, event | category | flops | bytes accessed | tf_op | source)
XLA Modules:
  0.0 2166.7 jit_solution(13448815169079959396)
XLA Ops:
  14.9 32.7 %all-gather = bf16[1,2,768]{1,0,2:T(2,128)(2,1)S(1)} all-gather(bf16[1,2,96]{1,0,2:T(2,128)(2,1)S(1)} %copy.71), channel_id=2, replica_groups=mesh['dp'=8,'tensor'=4] {'dp'}, dimensions={2}, use_global_device_ids=true | all-gather | bytes 3456 | tf_op jit(solution)/shard_map/all_gather | solution.py:152
  53.2 31.1 %all-gather.1 = bf16[1,4,768]{1,0,2:T(2,128)(2,1)S(1)} all-gather(bf16[1,4,96]{1,0,2:T(2,128)(2,1)S(1)} %copy.72), channel_id=3, replica_groups=mesh['dp'=8,'tensor'=4] {'dp'}, dimensions={2}, use_global_device_ids=true | all-gather | bytes 6912 | tf_op jit(solution)/shard_map/all_gather | solution.py:153
  99.8 30.6 %all-gather.3 = bf16[1,2,192]{1,0,2:T(2,128)(2,1)S(1)} all-gather(bf16[1,2,24]{1,0,2:T(2,128)(2,1)S(1)} %copy.74), channel_id=5, replica_groups=mesh['dp'=8,'tensor'=4] {'dp'}, dimensions={2}, use_global_device_ids=true | all-gather | bytes 864 | tf_op jit(solution)/shard_map/all_gather | solution.py:154
  134.7 32.8 %all-gather.4 = bf16[1,192,768]{1,0,2:T(2,128)(2,1)S(1)} all-gather(bf16[1,192,96]{1,0,2:T(2,128)(2,1)S(1)} %copy.75), channel_id=6, replica_groups=mesh['dp'=8,'tensor'=4] {'dp'}, dimensions={2}, use_global_device_ids=true | all-gather | bytes 331776 | tf_op jit(solution)/shard_map/all_gather | solution.py:149
  169.1 32.9 %all-gather.2 = bf16[1,768,3,192]{3,2,0,1:T(4,128)(2,1)S(1)} all-gather(bf16[1,96,3,192]{3,2,0,1:T(4,128)(2,1)S(1)} %copy.73), channel_id=4, replica_groups=mesh['dp'=8,'tensor'=4] {'dp'}, dimensions={1}, use_global_device_ids=true | all-gather | bytes 995328 | tf_op jit(solution)/shard_map/all_gather | solution.py:148
  218.3 336.9 %while.52 = (s32[]{:T(128)}, bf16[8,512,3,64]{1,3,2,0:T(8,128)(2,1)}, f32[8,3,512]{2,1,0:T(4,128)}, s32[8]{0:T(128)S(1)}, s32[]{:T(128)}, /*index=5*/s32[]{:T(12...) while((s32[]{:T(128)}, ...), condition=%wide.region_5.6_spmd.clone.clone, body=%wide.region_2.5_spmd.clone.clone.sunk | while | flops 1692513280 | bytes 93781200 | solution.py:63
  247.3 12.7 fusion.155
  289.3 12.7 fusion.155
  373.3 12.7 fusion.155
  567.5 57.1 %reduce-scatter.18.cloned.1.call-done = bf16[1024,768]{1,0:T(8,128)(2,1)} async-done(((bf16[4096,768]{1,0:T(8,128)(2,1)}), bf16[1024,768]{1,0:T(8,128)(2,1)}) %reduce-scatter.18.cloned.1.call-update) | async-done | bytes 1572880 | tf_op jit(solution)/shard_map/reduce_scatter | solution.py:179
  631.9 21.5 all-reduce
  668.2 34.3 %all-gather.23.cloned.1.call-done = bf16[1,768,768]{2,1,0:T(8,128)(2,1)} async-done(((bf16[1,96,768]{2,1,0:T(8,128)(2,1)}), bf16[1,768,768]{2,1,0:T(8,128)(2,1)}) %all-gather.23.cloned.1.call-update) | async-done | bytes 1179664 | tf_op jit(solution)/shard_map/all_gather | solution.py:150
  702.4 47.0 %all-gather.17.cloned.1.call-done = bf16[4096,768]{1,0:T(8,128)(2,1)} async-done(((bf16[1024,768]{1,0:T(8,128)(2,1)}), bf16[4096,768]{1,0:T(8,128)(2,1)}) %all-gather.17.cloned.1.call-update) | async-done | bytes 6291472 | tf_op jit(solution)/shard_map/all_gather | solution.py:188
  749.4 24.4 %convert_reduce_fusion = (f32[768]{0:T(1024)}, bf16[4096,768]{1,0:T(8,128)(2,1)S(1)}, bf16[4096,768]{1,0:T(8,128)(2,1)}) fusion(f32[768]{0:T(1024)S(1)} %convert_element_type.197, f32[768,4096]{0,1:T(8,128)} %fusion.84, bf16[4096,768]{1,0:T(8,128)(2,1)} %all-gather.17.cloned.1.call-done, bf16[1,768,768]{2,1,0:T(8,128)(2,1)} %all-gather.23.cloned.1.call-done), kind=kOutput, calls=%fused_computation.80 | convolution fusion | flops 4923063296 | bytes 32643072 | tf_op jit(solution)/shard_map/dot_general | solution.py:189
  793.7 48.8 %reduce-scatter.22.cloned.1.call-done = bf16[1024,768]{1,0:T(8,128)(2,1)} async-done(((bf16[4096,768]{1,0:T(8,128)(2,1)}), bf16[1024,768]{1,0:T(8,128)(2,1)}) %reduce-scatter.22.cloned.1.call-update) | async-done | bytes 1572880 | tf_op jit(solution)/shard_map/reduce_scatter | solution.py:208
  846.1 57.2 %reduce-scatter.20.cloned.1.call-done = bf16[1024,768]{1,0:T(8,128)(2,1)} async-done(((bf16[4096,768]{1,0:T(8,128)(2,1)}), bf16[1024,768]{1,0:T(8,128)(2,1)}) %reduce-scatter.20.cloned.1.call-update) | async-done | bytes 1572880 | tf_op jit(solution)/shard_map/reduce_scatter | solution.py:194
  910.4 46.3 %all-gather.21.cloned.1.call-done = bf16[4096,768]{1,0:T(8,128)(2,1)} async-done(((bf16[1024,768]{1,0:T(8,128)(2,1)}), bf16[4096,768]{1,0:T(8,128)(2,1)}) %all-gather.21.cloned.1.call-update) | async-done | bytes 6291472 | tf_op jit(solution)/shard_map/all_gather | solution.py:222
  963.9 708.4 %while.53 = (s32[]{:T(128)}, f32[4096,3,64]{0,2,1:T(8,128)}, f32[4096,3,64]{0,2,1:T(8,128)}, bf16[8,512,3,64]{1,3,2,0:T(8,128)(2,1)}, bf16[8,512,3,64]{1,3,2,0:T...) while((s32[]{:T(128)}, f32[4096,3,64]{0,2,1:T(8,128)}, ...), condition=%wide.region_15.16_spmd.clone.clone, body=%wide.region_13.15_spmd.clone.clone.sunk | while | flops 4131238912 | bytes 224058640 | solution.py:110
  993.5 17.8 multiply_reduce_fusion.3
  1011.3 21.8 %multiply_convert_fusion.3 = bf16[3,512,4096]{2,1,0:T(8,128)(2,1)} fusion(f32[3,512,4096]{2,1,0:T(8,128)} %get-tuple-element.670, f32[3,512,4096]{2,1,0:T(8,128)} %fusion.165, f32[3,512]{1,0:T(4,128)S(1)} %get-tuple-element.671, f32[3,512]{1,0:T(4,128)S(1)} %dynamic-slice_bitcast_fusion.2, pred[512,4096]{1,0:T(8,128)(4,1)} %copy-done.2), kind=kLoop, calls=%fused_computation.25.clone.1 | loop fusion | flops 37748736 | bytes 65024000 | tf_op jit(solution)/shard_map/while/body/eval_jaxpr/while/body/eval_jaxpr/convert_element_type | solution.py:94
  1067.9 13.4 fusion.169
  1081.4 17.8 multiply_reduce_fusion.3
  1099.1 21.8 %multiply_convert_fusion.3 = bf16[3,512,4096]{2,1,0:T(8,128)(2,1)} fusion(f32[3,512,4096]{2,1,0:T(8,128)} %get-tuple-element.670, f32[3,512,4096]{2,1,0:T(8,128)} %fusion.165, f32[3,512]{1,0:T(4,128)S(1)} %get-tuple-element.671, f32[3,512]{1,0:T(4,128)S(1)} %dynamic-slice_bitcast_fusion.2, pred[512,4096]{1,0:T(8,128)(4,1)} %copy-done.2), kind=kLoop, calls=%fused_computation.25.clone.1 | loop fusion | flops 37748736 | bytes 65024000 | tf_op jit(solution)/shard_map/while/body/eval_jaxpr/while/body/eval_jaxpr/convert_element_type | solution.py:94
  1156.7 13.4 fusion.169
  1170.1 17.8 multiply_reduce_fusion.3
  1187.9 21.8 %multiply_convert_fusion.3 = bf16[3,512,4096]{2,1,0:T(8,128)(2,1)} fusion(f32[3,512,4096]{2,1,0:T(8,128)} %get-tuple-element.670, f32[3,512,4096]{2,1,0:T(8,128)} %fusion.165, f32[3,512]{1,0:T(4,128)S(1)} %get-tuple-element.671, f32[3,512]{1,0:T(4,128)S(1)} %dynamic-slice_bitcast_fusion.2, pred[512,4096]{1,0:T(8,128)(4,1)} %copy-done.2), kind=kLoop, calls=%fused_computation.25.clone.1 | loop fusion | flops 37748736 | bytes 65024000 | tf_op jit(solution)/shard_map/while/body/eval_jaxpr/while/body/eval_jaxpr/convert_element_type | solution.py:94
  1245.4 13.4 fusion.169
  1258.8 17.8 multiply_reduce_fusion.3
  1276.6 21.8 %multiply_convert_fusion.3 = bf16[3,512,4096]{2,1,0:T(8,128)(2,1)} fusion(f32[3,512,4096]{2,1,0:T(8,128)} %get-tuple-element.670, f32[3,512,4096]{2,1,0:T(8,128)} %fusion.165, f32[3,512]{1,0:T(4,128)S(1)} %get-tuple-element.671, f32[3,512]{1,0:T(4,128)S(1)} %dynamic-slice_bitcast_fusion.2, pred[512,4096]{1,0:T(8,128)(4,1)} %copy-done.2), kind=kLoop, calls=%fused_computation.25.clone.1 | loop fusion | flops 37748736 | bytes 65024000 | tf_op jit(solution)/shard_map/while/body/eval_jaxpr/while/body/eval_jaxpr/convert_element_type | solution.py:94
  1334.1 13.4 fusion.169
  1347.6 17.8 multiply_reduce_fusion.3
  1365.3 21.8 %multiply_convert_fusion.3 = bf16[3,512,4096]{2,1,0:T(8,128)(2,1)} fusion(f32[3,512,4096]{2,1,0:T(8,128)} %get-tuple-element.670, f32[3,512,4096]{2,1,0:T(8,128)} %fusion.165, f32[3,512]{1,0:T(4,128)S(1)} %get-tuple-element.671, f32[3,512]{1,0:T(4,128)S(1)} %dynamic-slice_bitcast_fusion.2, pred[512,4096]{1,0:T(8,128)(4,1)} %copy-done.2), kind=kLoop, calls=%fused_computation.25.clone.1 | loop fusion | flops 37748736 | bytes 65024000 | tf_op jit(solution)/shard_map/while/body/eval_jaxpr/while/body/eval_jaxpr/convert_element_type | solution.py:94
  1422.9 13.4 fusion.169
  1436.3 17.8 multiply_reduce_fusion.3
  1454.0 21.8 %multiply_convert_fusion.3 = bf16[3,512,4096]{2,1,0:T(8,128)(2,1)} fusion(f32[3,512,4096]{2,1,0:T(8,128)} %get-tuple-element.670, f32[3,512,4096]{2,1,0:T(8,128)} %fusion.165, f32[3,512]{1,0:T(4,128)S(1)} %get-tuple-element.671, f32[3,512]{1,0:T(4,128)S(1)} %dynamic-slice_bitcast_fusion.2, pred[512,4096]{1,0:T(8,128)(4,1)} %copy-done.2), kind=kLoop, calls=%fused_computation.25.clone.1 | loop fusion | flops 37748736 | bytes 65024000 | tf_op jit(solution)/shard_map/while/body/eval_jaxpr/while/body/eval_jaxpr/convert_element_type | solution.py:94
  1511.6 13.4 fusion.169
  1525.0 17.8 multiply_reduce_fusion.3
  1542.8 21.8 %multiply_convert_fusion.3 = bf16[3,512,4096]{2,1,0:T(8,128)(2,1)} fusion(f32[3,512,4096]{2,1,0:T(8,128)} %get-tuple-element.670, f32[3,512,4096]{2,1,0:T(8,128)} %fusion.165, f32[3,512]{1,0:T(4,128)S(1)} %get-tuple-element.671, f32[3,512]{1,0:T(4,128)S(1)} %dynamic-slice_bitcast_fusion.2, pred[512,4096]{1,0:T(8,128)(4,1)} %copy-done.2), kind=kLoop, calls=%fused_computation.25.clone.1 | loop fusion | flops 37748736 | bytes 65024000 | tf_op jit(solution)/shard_map/while/body/eval_jaxpr/while/body/eval_jaxpr/convert_element_type | solution.py:94
  1600.3 13.4 fusion.169
  1613.7 17.8 multiply_reduce_fusion.3
  1631.5 21.8 %multiply_convert_fusion.3 = bf16[3,512,4096]{2,1,0:T(8,128)(2,1)} fusion(f32[3,512,4096]{2,1,0:T(8,128)} %get-tuple-element.670, f32[3,512,4096]{2,1,0:T(8,128)} %fusion.165, f32[3,512]{1,0:T(4,128)S(1)} %get-tuple-element.671, f32[3,512]{1,0:T(4,128)S(1)} %dynamic-slice_bitcast_fusion.2, pred[512,4096]{1,0:T(8,128)(4,1)} %copy-done.2), kind=kLoop, calls=%fused_computation.25.clone.1 | loop fusion | flops 37748736 | bytes 65024000 | tf_op jit(solution)/shard_map/while/body/eval_jaxpr/while/body/eval_jaxpr/convert_element_type | solution.py:94
  1696.4 50.5 %reduce-scatter.24.cloned.1.call-done = bf16[1024,768]{1,0:T(8,128)(2,1)} async-done(((bf16[4096,768]{1,0:T(8,128)(2,1)}), bf16[1024,768]{1,0:T(8,128)(2,1)}) %reduce-scatter.24.cloned.1.call-update) | async-done | bytes 1572880 | tf_op jit(solution)/shard_map/reduce_scatter | solution.py:241
  1790.6 21.7 %all-reduce.3 = (f32[2,192]{1,0:T(2,128)S(1)}, f32[768]{0:T(1024)S(1)}) all-reduce(f32[2,192]{1,0:T(2,128)S(1)} %pad_maximum_fusion.5, f32[768]{0:T(1024)S(1)} %copy-done.44), channel_id=20, replica_groups=mesh['dp'=8,'tensor'=4] {'dp'}, use_global_device_ids=true, to_apply=%region_35.36.clone | all-reduce | flops 1152 | bytes 9216
  1815.1 61.6 %reduce-scatter.34.cloned.1.call-done = f32[96,2]{1,0:T(8,128)} async-done(((f32[768,2]{1,0:T(8,128)}), f32[96,2]{1,0:T(8,128)}) %reduce-scatter.34.cloned.1.call-update) | async-done | bytes 784
  1877.6 63.2 %reduce-scatter.36.cloned.1.call-done = f32[96,4]{1,0:T(8,128)} async-done(((f32[768,4]{1,0:T(8,128)}), f32[96,4]{1,0:T(8,128)}) %reduce-scatter.36.cloned.1.call-update) | async-done | bytes 1552
  1947.9 66.1 %reduce-scatter.28.cloned.1.call-done = f32[96,768]{1,0:T(8,128)} async-done(((f32[768,768]{1,0:T(8,128)}), f32[96,768]{1,0:T(8,128)}) %reduce-scatter.28.cloned.1.call-update) | async-done | bytes 294928 | tf_op jit(solution)/shard_map/reduce_scatter | solution.py:268
  2014.0 72.7 %reduce-scatter.30.cloned.1.call-done = f32[768,96]{0,1:T(8,128)} async-done(((f32[768,768]{0,1:T(8,128)}), f32[768,96]{0,1:T(8,128)}) %reduce-scatter.30.cloned.1.call-update) | async-done | bytes 294928 | tf_op jit(solution)/shard_map/reduce_scatter | solution.py:269
  2086.7 72.7 %reduce-scatter.26.cloned.1.call-done = f32[96,3,192]{2,0,1:T(8,128)} async-done(((f32[768,3,192]{2,0,1:T(8,128)}), f32[96,3,192]{2,0,1:T(8,128)}) %reduce-scatter.26.cloned.1.call-update) | async-done | bytes 221200 | tf_op jit(solution)/shard_map/reduce_scatter | solution.py:266
  (400 shorter events, 780.9 us)
Async XLA Ops:
  8.0 556.4 %copy-start = (bf16[12,768,96]{1,2,0:T(8,128)(2,1)S(1)}, bf16[12,768,96]{1,2,0:T(8,128)(2,1)}, u32[]{:S(2)}) copy-start(bf16[12,768,96]{1,2,0:T(8,128)(2,1)} %param.23) | copy-start | bytes 5308420
  8.0 196.0 %all-gather.15.cloned.1.call-start = ((), (), s32[]{:S(2)}) async-start(), calls=%async_computation.10 | async-start | bytes 7864320 | tf_op jit(solution)/shard_map/all_gather | solution.py:166
  11.9 83.7 %copy-start.27 = (f32[1024]{0:T(1024)}, f32[1024]{0:T(1024)S(1)}, u32[]{:S(2)}) copy-start(f32[1024]{0:T(1024)S(1)} %broadcast_multiply_fusion.1) | copy-start | bytes 12292
  11.9 83.7 %copy-start.3 = (bf16[1024,768]{1,0:T(8,128)(2,1)S(1)}, bf16[1024,768]{1,0:T(8,128)(2,1)}, u32[]{:S(2)}) copy-start(bf16[1024,768]{1,0:T(8,128)(2,1)} %param.16) | copy-start | bytes 4718596
  14.6 82.7 %copy-start.32 = (f32[1024]{0:T(1024)}, f32[1024]{0:T(1024)S(1)}, u32[]{:S(2)}) copy-start(f32[1024]{0:T(1024)S(1)} %fusion.93) | copy-start | bytes 12292
  53.2 44.1 %copy-start.30 = (f32[768]{0:T(1024)}, f32[768]{0:T(1024)S(1)}, u32[]{:S(2)}) copy-start(f32[768]{0:T(1024)S(1)} %get-tuple-element.466) | copy-start | bytes 9220
  97.4 527.2 %reduce-scatter.18.cloned.1.call-start = ((), (), s32[]{:S(2)}) async-start(), calls=%async_computation.11 | async-start | bytes 7864320 | tf_op jit(solution)/shard_map/reduce_scatter | solution.py:179
  235.3 11.9 copy-start.8
  277.3 11.9 copy-start.8
  319.3 11.9 copy-start.8
  361.4 11.9 copy-start.8
  403.4 11.9 copy-start.8
  445.4 11.9 copy-start.8
  487.4 11.9 copy-start.8
  529.5 11.9 copy-start.8
  564.4 60.3 %copy-start.4 = (bf16[1024,768]{1,0:T(8,128)(2,1)S(1)}, bf16[1024,768]{1,0:T(8,128)(2,1)}, u32[]{:S(2)}) copy-start(bf16[1024,768]{1,0:T(8,128)(2,1)} %param.16) | copy-start | bytes 4718596
  564.4 60.3 %copy-start.29 = (f32[768]{0:T(1024)S(1)}, f32[768]{0:T(1024)}, u32[]{:S(2)}) copy-start(f32[768]{0:T(1024)} %get-tuple-element.464) | copy-start | bytes 9220
  564.4 89.0 %all-gather.25.cloned.1.call-start = ((), (), s32[]{:S(2)}) async-start(), calls=%async_computation.22 | async-start | bytes 1327104 | tf_op jit(solution)/shard_map/all_gather | solution.py:151
  565.2 92.9 %all-gather.19.cloned.1.call-start = ((), (), s32[]{:S(2)}) async-start(), calls=%async_computation.14 | async-start | bytes 7864320 | tf_op jit(solution)/shard_map/all_gather | solution.py:200
  565.8 136.7 %all-gather.23.cloned.1.call-start = ((), (), s32[]{:S(2)}) async-start(), calls=%async_computation.21 | async-start | bytes 1327104 | tf_op jit(solution)/shard_map/all_gather | solution.py:150
  567.4 182.0 %all-gather.17.cloned.1.call-start = ((), (), s32[]{:S(2)}) async-start(), calls=%async_computation.12 | async-start | bytes 7864320 | tf_op jit(solution)/shard_map/all_gather | solution.py:188
  629.7 212.7 %reduce-scatter.22.cloned.1.call-start = ((), (), s32[]{:S(2)}) async-start(), calls=%async_computation.15 | async-start | bytes 7864320 | tf_op jit(solution)/shard_map/reduce_scatter | solution.py:208
  749.4 27.0 %copy-start.46 = (bf16[1,768,768]{2,1,0:T(8,128)(2,1)S(1)}, bf16[1,768,768]{2,1,0:T(8,128)(2,1)}, u32[]{:S(2)}) copy-start(bf16[1,768,768]{2,1,0:T(8,128)(2,1)} %all-gather.23.cloned.1.call-done) | copy-start | bytes 3538948
  783.9 119.3 %reduce-scatter.20.cloned.1.call-start = ((), (), s32[]{:S(2)}) async-start(), calls=%async_computation.13 | async-start | bytes 7864320 | tf_op jit(solution)/shard_map/reduce_scatter | solution.py:194
  793.6 109.7 %copy-start.39 = (f32[768]{0:T(1024)S(1)}, f32[768]{0:T(1024)}, u32[]{:S(2)}) copy-start(f32[768]{0:T(1024)} %get-tuple-element.462) | copy-start | bytes 9220
  793.6 163.0 %all-gather.21.cloned.1.call-start = ((), (), s32[]{:S(2)}) async-start(), calls=%async_computation.16 | async-start | bytes 7864320 | tf_op jit(solution)/shard_map/all_gather | solution.py:222
  907.6 49.0 %copy-start.25 = (bf16[1,192,768]{2,1,0:T(8,128)(2,1)S(1)}, bf16[1,192,768]{2,1,0:T(8,128)(2,1)}, u32[]{:S(2)}) copy-start(bf16[1,192,768]{2,1,0:T(8,128)(2,1)} %copy.55) | copy-start | bytes 884740
  910.3 836.6 %reduce-scatter.24.cloned.1.call-start = ((), (), s32[]{:S(2)}) async-start(), calls=%async_computation.17 | async-start | bytes 7864320 | tf_op jit(solution)/shard_map/reduce_scatter | solution.py:241
  969.8 11.3 copy-start.2
  1056.6 11.3 copy-start.2
  1234.1 11.3 copy-start.2
  1322.8 11.3 copy-start.2
  1411.5 11.3 copy-start.2
  1500.3 11.3 copy-start.2
  1688.5 124.9 %reduce-scatter.32.cloned.1.call-start = ((), (), s32[]{:S(2)}) async-start(), calls=%async_computation.23 | async-start | bytes 884736
  1689.9 56.9 %copy-start.5 = (bf16[1024,768]{1,0:T(8,128)(2,1)S(1)}, bf16[1024,768]{1,0:T(8,128)(2,1)}, u32[]{:S(2)}) copy-start(bf16[1024,768]{1,0:T(8,128)(2,1)} %param.16) | copy-start | bytes 4718596
  1689.9 56.9 %copy-start.28 = (f32[1024]{0:T(1024)S(1)}, f32[1024]{0:T(1024)}, u32[]{:S(2)}) copy-start(f32[1024]{0:T(1024)} %copy-done.27) | copy-start | bytes 12292
  1690.0 56.9 %copy-start.31 = (f32[768]{0:T(1024)S(1)}, f32[768]{0:T(1024)}, u32[]{:S(2)}) copy-start(f32[768]{0:T(1024)} %copy-done.30) | copy-start | bytes 9220
  1696.3 53.2 %copy-start.38 = (f32[1024]{0:T(1024)S(1)}, f32[1024]{0:T(1024)}, u32[]{:S(2)}) copy-start(f32[1024]{0:T(1024)} %copy-done.37) | copy-start | bytes 12292
  1696.3 53.3 %copy-start.33 = (f32[1024]{0:T(1024)S(1)}, f32[1024]{0:T(1024)}, u32[]{:S(2)}) copy-start(f32[1024]{0:T(1024)} %copy-done.32) | copy-start | bytes 12292
  1696.3 56.4 %copy-start.15 = (bf16[1024,768]{1,0:T(8,128)(2,1)S(1)}, bf16[1024,768]{1,0:T(8,128)(2,1)}, u32[]{:S(2)}) copy-start(bf16[1024,768]{1,0:T(8,128)(2,1)} %param.17) | copy-start | bytes 4718596
  1696.4 56.4 %copy-start.36 = (f32[1024]{0:T(1024)S(1)}, f32[1024]{0:T(1024)}, u32[]{:S(2)}) copy-start(f32[1024]{0:T(1024)} %copy-done.35) | copy-start | bytes 12292
  1696.4 180.4 %reduce-scatter.34.cloned.1.call-start = ((), (), s32[]{:S(2)}) async-start(), calls=%async_computation.24 | async-start | bytes 442368
  1756.4 184.4 %reduce-scatter.36.cloned.1.call-start = ((), (), s32[]{:S(2)}) async-start(), calls=%async_computation.25 | async-start | bytes 442368
  1757.5 256.5 %reduce-scatter.28.cloned.1.call-start = ((), (), s32[]{:S(2)}) async-start(), calls=%async_computation.19 | async-start | bytes 2654208 | tf_op jit(solution)/shard_map/reduce_scatter | solution.py:268
  1767.8 318.9 %reduce-scatter.30.cloned.1.call-start = ((), (), s32[]{:S(2)}) async-start(), calls=%async_computation.20 | async-start | bytes 2654208 | tf_op jit(solution)/shard_map/reduce_scatter | solution.py:269
  1778.2 381.2 %reduce-scatter.26.cloned.1.call-start = ((), (), s32[]{:S(2)}) async-start(), calls=%async_computation.18 | async-start | bytes 2654208 | tf_op jit(solution)/shard_map/reduce_scatter | solution.py:266
  1778.2 381.2 %copy-start.1 = (bf16[12,768,96]{1,2,0:T(8,128)(2,1)S(1)}, bf16[12,768,96]{1,2,0:T(8,128)(2,1)}, u32[]{:S(2)}) copy-start(bf16[12,768,96]{1,2,0:T(8,128)(2,1)} %param.23) | copy-start | bytes 5308420
  (30 other events, 112.4 us)
Sparse Core Ops, SparseCore 0:
  97.5 47.4 all-gather.14
  564.5 60.0 reduce-scatter.17
  784.0 58.3 reduce-scatter.21
  844.8 58.3 reduce-scatter.19
Sparse Core Ops, SparseCore 1:
  567.9 42.9 all-gather.24
  612.3 45.6 all-gather.18
  660.9 41.5 all-gather.22
  704.7 44.7 all-gather.16
  910.4 46.2 all-gather.20
  1688.6 58.2 reduce-scatter.23
  1750.1 62.6 reduce-scatter.31
  1816.2 60.5 reduce-scatter.33
  1880.2 60.5 reduce-scatter.35
  1945.3 68.7 reduce-scatter.27
  2018.3 68.3 reduce-scatter.29
  2091.2 68.2 reduce-scatter.25
where the time goes:
time: 2170 us
  matrix products  795 us (37%)
  waiting for transfers between devices  683 us (31%)
  other arithmetic  376 us (17%)
  blocking collectives  210 us (10%)
  local copies, waits for them, and re-layouts  70.6 us (3%)
    dot_general x16, matrix products, one_block(): jnp.einsum('qhe,khe->hqk', query_block, key_seq, preferred_element_type=j...  185 us
    convert_element_type x8, other arithmetic, one_block(): grad_scores = (weights * (grad_weights - centre)).astype(jnp.bfloat16)  174 us
    dot_general x8, matrix products, one_block(): jnp.einsum('qhe,khe->hqk', grad_block, value_seq, preferred_element_type=...  142 us
    unnamed x19, waiting for transfers between devices  126 us
    dot_general x8, matrix products, one_block(): jnp.einsum('hqk,qhe->khe', weights.astype(jnp.bfloat16), grad_block, pref...  106 us
    dot_general x8, matrix products, one_block(): jnp.einsum('hqk,khe->qhe', weights, value_seq, preferred_element_type=jnp...  102 us
    reduce_sum x8, other arithmetic, one_block(): summed = jnp.sum(raised, axis=-1, keepdims=True)  95.5 us
    dot_general x8, matrix products, one_block(): jnp.einsum('hqk,qhe->khe', grad_scores, query_block, preferred_element_ty...  75.4 us
  transfers between devices with their start and end apart: 16, of which 13 were waited for; matrix products, arithmetic and copies ran while one was open for 4% of the time, Pallas kernels for 0%

commit v1 on v0

v1 whole, which is shorter than its diff:
```python
import functools
import math

import jax
import jax.numpy as jnp
from jax import lax
from jax.experimental import pallas as pl
from jax.experimental.pallas import tpu as pltpu
from jax.sharding import PartitionSpec as P

HEAD_DIM = 64
SEQ_LEN = 4096
IMG = 256
EPSILON = 1e-05
LOG2E = 1.4426950408889634
BLOCK = 512
BLOCKS = SEQ_LEN // BLOCK
QUARTERS = 4
QUARTER = SEQ_LEN // QUARTERS
PER_QUARTER = QUARTER // BLOCK
PAIRS = BLOCKS * (BLOCKS + 1) // 2
F32 = jnp.float32
BF16 = jnp.bfloat16

NT = (((1,), (1,)), ((), ()))
NN = (((1,), (0,)), ((), ()))
TN = (((0,), (0,)), ((), ()))
CT = (((0,), (1,)), ((), ()))


def product(left, right, dims):
    return lax.dot_general(left, right, dims, preferred_element_type=F32)


def place(block, own):
    quarter = jnp.bitwise_xor(block // PER_QUARTER, own)
    return pl.multiple_of((quarter * PER_QUARTER + block % PER_QUARTER) * BLOCK, BLOCK)


def following(row, col, cross):
    wrap = col + 1 >= row + 1 + jnp.where(cross == row, 1, 0)
    return jnp.where(wrap, row + 1, row), jnp.where(wrap, 0, col + 1)


def crossing(start):
    low, high = start // BLOCK, (start + IMG - 1) // BLOCK
    cross = jnp.where(high > low, low, -1)
    return cross, PAIRS + jnp.where(cross >= 0, 1, 0)


def last_key(pos, start):
    return jnp.where((pos >= start) & (pos < start + IMG), start + (IMG - 1), pos)


def forward_kernel(
    info, q_ref, k_ref, v_ref, o_ref, lse_ref, k_rows, v_ones, s_a, s_b, top_a, top_b, top, total
):
    start, own = info[0], info[1]
    cross, pairs = crossing(start)

    def prepare(block, carry):
        at = pl.ds(pl.multiple_of(block * BLOCK, BLOCK), BLOCK)
        k_rows[at, :] = k_ref[0, 0, :, at].astype(F32).T.astype(BF16)
        return carry

    lax.fori_loop(0, BLOCKS, prepare, 0)
    v_ones[0:64, :] = v_ref[0, 0]
    v_ones[64:80, :] = jnp.ones((16, SEQ_LEN), BF16)
    total[...] = jnp.zeros_like(total)

    def score(row, col, dst, dst_top, masked):
        rows = pl.ds(place(jnp.minimum(row, BLOCKS - 1), own), BLOCK)
        s = product(k_rows[pl.ds(place(col, own), BLOCK), :], q_ref[0, 0, :, rows], NN)
        if masked:
            pos = row * BLOCK + lax.broadcasted_iota(jnp.int32, (1, BLOCK), 1)
            limit = last_key(pos, start) - col * BLOCK
            s = jnp.where(lax.broadcasted_iota(jnp.int32, (BLOCK, BLOCK), 0) <= limit, s, -1e30)
        dst[...] = s
        dst_top[...] = jnp.max(s, axis=0, keepdims=True)

    def step(src, src_top, dst, dst_top, col, next_row, next_col, masked):
        score(next_row, next_col, dst, dst_top, masked)
        old = jnp.where(col == 0, -1e30, top[...])
        new = jnp.maximum(old, src_top[...])
        p = jnp.exp2(src[...] - new).astype(BF16)
        mixed = product(v_ones[:, pl.ds(place(col, own), BLOCK)], p, NN)
        total[...] = total[...] * jnp.exp2(old - new) + mixed
        top[...] = new

    def half(src, src_top, dst, dst_top, row, col):
        next_row, next_col = following(row, col, cross)
        masked = next_col >= next_row

        @pl.when(masked)
        def _():
            step(src, src_top, dst, dst_top, col, next_row, next_col, True)

        @pl.when(jnp.logical_not(masked))
        def _():
            step(src, src_top, dst, dst_top, col, next_row, next_col, False)

        @pl.when(next_col == 0)
        def _():
            at = pl.ds(place(row, own), BLOCK)
            summed = total[64:65]
            o_ref[:, at] = (total[0:64] / summed).astype(BF16)
            lse_ref[:, at] = top[...] + jnp.log2(summed)

        return next_row, next_col

    score(0, 0, s_a, top_a, True)

    def both(turn, carry):
        row, col = half(s_a, top_a, s_b, top_b, *carry)
        return half(s_b, top_b, s_a, top_a, row, col)

    row, col = lax.fori_loop(0, pairs // 2, both, (jnp.int32(0), jnp.int32(0)))

    @pl.when(pairs % 2 == 1)
    def _():
        half(s_a, top_a, s_b, top_b, row, col)


def head_spec(head, part):
    return pl.BlockSpec((1, 1, HEAD_DIM, SEQ_LEN), lambda i, info: (head, part, 0, 0))


def attend_forward(info, qkv, head):
    whole = lambda rows: pl.BlockSpec((rows, SEQ_LEN), lambda i, info: (0, 0))
    return pl.pallas_call(
        forward_kernel,
        grid_spec=pltpu.PrefetchScalarGridSpec(
            num_scalar_prefetch=1,
            grid=(1,),
            in_specs=[head_spec(head, part) for part in range(3)],
            out_specs=[whole(HEAD_DIM), whole(1)],
            scratch_shapes=[
                pltpu.VMEM((SEQ_LEN, HEAD_DIM), BF16),
                pltpu.VMEM((80, SEQ_LEN), BF16),
                pltpu.VMEM((BLOCK, BLOCK), F32),
                pltpu.VMEM((BLOCK, BLOCK), F32),
                pltpu.VMEM((1, BLOCK), F32),
                pltpu.VMEM((1, BLOCK), F32),
                pltpu.VMEM((1, BLOCK), F32),
                pltpu.VMEM((80, BLOCK), F32),
            ],
        ),
        out_shape=[
            jax.ShapeDtypeStruct((HEAD_DIM, SEQ_LEN), BF16),
            jax.ShapeDtypeStruct((1, SEQ_LEN), F32),
        ],
        cost_estimate=pl.CostEstimate(
            flops=18_000_000_000, bytes_accessed=2_200_000, transcendentals=9_000_000
        ),
        name="attend_forward",
    )(info, qkv, qkv, qkv)


def pieces(values):
    high = values.astype(BF16).astype(F32)
    rest = values - high
    middle = rest.astype(BF16).astype(F32)
    return [high, middle, (rest - middle).astype(BF16).astype(F32)]


def backward_kernel(
    info, q_ref, k_ref, v_ref, g_ref, o_ref, lse_ref, d_ref,
    q_wide, k_wide, v_wide, g_wide, p_a, ds_a, p_b, ds_b, dq, dk, dv,
):
    start, own = info[0], info[1]
    cross, pairs = crossing(start)

    def prepare(block, carry):
        at = pl.ds(pl.multiple_of(block * BLOCK, BLOCK), BLOCK)
        ones = [jnp.ones((1, BLOCK), F32)] * 3

        def widen(columns, rows):
            rest = jnp.zeros((HEAD_DIM - 3, BLOCK), F32)
            return jnp.concatenate([columns.astype(F32)] + rows + [rest], axis=0).T.astype(BF16)

        grad = g_ref[:, at]
        centre = jnp.sum(grad.astype(F32) * o_ref[:, at].astype(F32), axis=0, keepdims=True)
        q_wide[at, :] = widen(q_ref[0, 0, :, at], pieces(-lse_ref[:, at]))
        k_wide[at, :] = widen(k_ref[0, 0, :, at], ones)
        v_wide[at, :] = widen(v_ref[0, 0, :, at], ones)
        g_wide[at, :] = widen(grad, pieces(-centre))
        return carry

    lax.fori_loop(0, BLOCKS, prepare, 0)
    dq[...] = jnp.zeros_like(dq)
    dk[...] = jnp.zeros_like(dk)
    dv[...] = jnp.zeros_like(dv)

    def score(row, col, p_dst, ds_dst, masked):
        rows = pl.ds(place(jnp.minimum(row, BLOCKS - 1), own), BLOCK)
        cols = pl.ds(place(col, own), BLOCK)
        s = product(q_wide[rows, :], k_wide[cols, :], NT)
        grad_p = product(g_wide[rows, :], v_wide[cols, :], NT)
        if masked:
            pos = row * BLOCK + lax.broadcasted_iota(jnp.int32, (BLOCK, 1), 0)
            limit = last_key(pos, start) - col * BLOCK
            s = jnp.where(lax.broadcasted_iota(jnp.int32, (BLOCK, BLOCK), 1) <= limit, s, -1e30)
        p = jnp.exp2(s)
        p_dst[...] = p.astype(BF16)
        ds_dst[...] = (p * grad_p).astype(BF16)

    def step(p, ds, p_dst, ds_dst, row, col, next_row, next_col, masked):
        score(next_row, next_col, p_dst, ds_dst, masked)
        rows = pl.ds(place(row, own), BLOCK)
        cols = pl.ds(place(col, own), BLOCK)
        dv[:, cols] += product(g_ref[:, rows], p[...], NN)
        dk[:, cols] += product(q_ref[0, 0, :, rows], ds[...], NN)
        dq[:, rows] += product(k_ref[0, 0, :, cols], ds[...], NT)

    def half(p, ds, p_dst, ds_dst, row, col):
        next_row, next_col = following(row, col, cross)
        masked = next_col >= next_row

        @pl.when(masked)
        def _():
            step(p, ds, p_dst, ds_dst, row, col, next_row, next_col, True)

        @pl.when(jnp.logical_not(masked))
        def _():
            step(p, ds, p_dst, ds_dst, row, col, next_row, next_col, False)

        return next_row, next_col

    score(0, 0, p_a, ds_a, True)

    def both(turn, carry):
        row, col = half(p_a, ds_a, p_b, ds_b, *carry)
        return half(p_b, ds_b, p_a, ds_a, row, col)

    row, col = lax.fori_loop(0, pairs // 2, both, (jnp.int32(0), jnp.int32(0)))

    @pl.when(pairs % 2 == 1)
    def _():
        half(p_a, ds_a, p_b, ds_b, row, col)

    d_ref[0:64, :] = (dq[...] * 0.125).astype(BF16)
    d_ref[64:128, :] = (dk[...] * (1.0 / LOG2E)).astype(BF16)
    d_ref[128:192, :] = dv[...].astype(BF16)


def attend_backward(info, qkv, grad, out, lse, head):
    whole = lambda rows: pl.BlockSpec((rows, SEQ_LEN), lambda i, info: (0, 0))
    return pl.pallas_call(
        backward_kernel,
        grid_spec=pltpu.PrefetchScalarGridSpec(
            num_scalar_prefetch=1,
            grid=(1,),
            in_specs=[head_spec(head, part) for part in range(3)]
            + [whole(HEAD_DIM), whole(HEAD_DIM), whole(1)],
            out_specs=whole(3 * HEAD_DIM),
            scratch_shapes=[pltpu.VMEM((SEQ_LEN, 128), BF16)] * 4
            + [pltpu.VMEM((BLOCK, BLOCK), BF16)] * 4
            + [pltpu.VMEM((HEAD_DIM, SEQ_LEN), F32)] * 3,
        ),
        out_shape=jax.ShapeDtypeStruct((3 * HEAD_DIM, SEQ_LEN), BF16),
        cost_estimate=pl.CostEstimate(
            flops=32_000_000_000, bytes_accessed=4_500_000, transcendentals=9_000_000
        ),
        name="attend_backward",
    )(info, qkv, qkv, qkv, grad, out, lse)


def normalise(values):
    centred = values - jnp.mean(values, axis=-1, keepdims=True)
    scale = lax.rsqrt(jnp.mean(centred * centred, axis=-1, keepdims=True) + EPSILON)
    return centred * scale, scale


def normalise_back(grad, unit, scale):
    return scale * (
        grad
        - jnp.mean(grad, axis=-1, keepdims=True)
        - unit * jnp.mean(grad * unit, axis=-1, keepdims=True)
    )


def gelu_both(u):
    inner = 0.7978845608028654 * (u + 0.044715 * u * u * u)
    bent = jnp.tanh(inner)
    slope = 0.7978845608028654 * (1.0 + 3 * 0.044715 * u * u)
    return 0.5 * u * (1.0 + bent), 0.5 * (1.0 + bent) + 0.5 * u * (1.0 - bent * bent) * slope


def swap(values, mask):
    return lax.ppermute(values, "tensor", [(i, i ^ mask) for i in range(QUARTERS)])


def gather_dp(part, count):
    if count > 8:
        return lax.all_gather(part, "dp", axis=0, tiled=False)
    ring = [part] + [
        lax.ppermute(part, "dp", [((i + k) % count, i) for i in range(count)])
        for k in range(1, count)
    ]
    twice = jnp.stack(ring + ring)
    first = lax.rem(count - lax.axis_index("dp"), count)
    return lax.dynamic_slice_in_dim(twice, first, count, 0)


def local(
    n_dp,
    tokens,
    cotangent,
    tie_index,
    image_start,
    qkv_bank,
    out_bank,
    up_bank,
    down_bank,
    gain_bank,
    shift_bank,
    head_bias_bank,
    hidden_bias_bank,
):
    own = lax.axis_index("tensor")
    chosen = tie_index[0]
    pick = lambda bank: lax.dynamic_index_in_dim(bank, chosen, 0, keepdims=False)
    width = tokens.shape[1]
    rows = qkv_bank.shape[1]
    local_width = qkv_bank.shape[3]
    heads = local_width // HEAD_DIM
    qkv_cols = 3 * local_width
    info = jnp.stack([image_start[0], own]).astype(jnp.int32)

    qkv_part = (
        pick(qkv_bank).reshape(rows, 3, heads, HEAD_DIM).transpose(0, 2, 1, 3).reshape(rows, qkv_cols)
    )
    out_part = pick(out_bank).T
    up_part = pick(up_bank)
    down_part = pick(down_bank).T
    gain_part = pick(gain_bank)
    shift_part = pick(shift_bank)
    head_part = pick(head_bias_bank)
    hidden_part = pick(hidden_bias_bank)
    few = head_part.shape[1]
    hidden_cols = up_part.shape[1]

    near = swap(tokens, 1)
    far = swap(tokens, 2)
    far_near = swap(far, 1)

    small = jnp.concatenate([gain_part.reshape(-1), shift_part.reshape(-1), head_part.reshape(-1)])
    small_rows = -(-small.shape[0] // qkv_cols)
    pad_rows = -(-small_rows // 16) * 16
    small = jnp.pad(small, (0, pad_rows * qkv_cols - small.shape[0])).reshape(pad_rows, qkv_cols)
    gathered = gather_dp(jnp.concatenate([qkv_part, small]), n_dp)
    w_qkv = gathered[:, :rows].reshape(width, qkv_cols)
    small = gathered[:, rows:].reshape(n_dp, -1).astype(F32)
    gains = small[:, : 2 * rows].reshape(n_dp, 2, rows).transpose(1, 0, 2).reshape(2, width)
    shifts = (
        small[:, 2 * rows : 6 * rows].reshape(n_dp, 4, rows).transpose(1, 0, 2).reshape(4, width)
    )
    head_bias = (
        small[:, 6 * rows : 6 * rows + 2 * few]
        .reshape(n_dp, 2, few)
        .transpose(1, 0, 2)
        .reshape(2, heads, 1, HEAD_DIM)
    )

    bank_part = jnp.concatenate(
        [
            up_part,
            down_part,
            out_part,
            qkv_part,
            jnp.pad(hidden_part.reshape(rows, -1), ((0, 0), (0, 127)))
            if hidden_part.shape[0] == rows
            else jnp.zeros((rows, 128), BF16),
        ],
        axis=1,
    )
    bank = lax.all_gather(bank_part, ("tensor", "dp"), axis=0, tiled=True)
    c_down, c_out, c_qkv, c_bias = (
        hidden_cols,
        2 * hidden_cols,
        2 * hidden_cols + local_width,
        2 * hidden_cols + local_width + qkv_cols,
    )
    block_of = lambda x: jnp.bitwise_xor(own, x) * width
    out_t = jnp.concatenate(
        [
            lax.dynamic_slice(bank, (block_of(x), c_out), (width, local_width))
            for x in range(QUARTERS)
        ],
        axis=1,
    )
    qkv_t = [
        lax.dynamic_slice(bank, (block_of(x), c_qkv), (width, qkv_cols)) for x in range(QUARTERS)
    ]

    zero_bias = jnp.zeros((heads, 1, HEAD_DIM), F32)
    bias = jnp.concatenate([head_bias[0], zero_bias, head_bias[1]], axis=1)[..., None]
    scale = jnp.array([LOG2E / 8.0, 1.0, 1.0], F32).reshape(1, 3, 1, 1)
    normed, projected = [], []
    for part in (tokens, near, far, far_near):
        unit, _ = normalise(part.astype(F32))
        rounded = (unit * gains[0] + shifts[0]).astype(BF16)
        flat = product(w_qkv, rounded, CT).reshape(heads, 3, HEAD_DIM, QUARTER)
        normed.append(rounded)
        projected.append(((flat + bias) * scale).astype(BF16))
    qkv = jnp.concatenate(projected, axis=3)
    normed = jnp.concatenate(normed, axis=0)

    outs, lses, mixed = [], [], [[None] * heads for _ in range(QUARTERS)]
    for head in range(heads):
        out, lse = attend_forward(info, qkv, head)
        outs.append(out)
        lses.append(lse)
        for x in range(QUARTERS):
            part = out[:, x * QUARTER : (x + 1) * QUARTER]
            mixed[x][head] = swap(part, x) if x else part
    mixed = jnp.concatenate([part for quarter in mixed for part in quarter], axis=0)

    inputs = tokens.astype(F32)
    middle = inputs + product(mixed, out_t, CT) + shifts[2]
    unit_two, scale_two = normalise(middle)
    normed_two = (unit_two * gains[1] + shifts[1]).astype(BF16)

    branch, grad_two = 0.0, 0.0
    grad_up, grad_down, grad_hidden = [], [], []
    for k in range(QUARTERS):
        w_up = bank[k * width : (k + 1) * width, :c_down]
        w_down = bank[k * width : (k + 1) * width, c_down:c_out]
        hidden_bias = bank[k * width : (k + 1) * width, c_bias].astype(F32)
        u = product(normed_two, w_up, NN) + hidden_bias
        value, slope = gelu_both(u)
        activ = value.astype(BF16)
        branch = branch + product(activ, w_down, NT)
        grad_u = (product(cotangent, w_down, NN) * slope).astype(BF16)
        grad_two = grad_two + product(grad_u, w_up, NT)
        grad_up.append(product(normed_two, grad_u, TN).astype(BF16))
        grad_down.append(product(cotangent, activ, TN).astype(BF16))
        grad_hidden.append(jnp.sum(grad_u, axis=0, dtype=F32))
    result = (middle + branch + shifts[3]).astype(BF16)

    grad_result = cotangent.astype(F32)
    grad_middle = grad_result + normalise_back(grad_two * gains[1], unit_two, scale_two)
    grad_low = grad_middle.astype(BF16)

    grad_out = product(grad_low, mixed, CT).astype(BF16)
    grads = jnp.concatenate(
        [
            jnp.concatenate(grad_up, axis=0),
            jnp.concatenate(grad_down, axis=0),
            jnp.zeros((QUARTERS * width, local_width), BF16),
        ],
        axis=1,
    )
    for x in range(QUARTERS):
        grads = lax.dynamic_update_slice(
            grads, grad_out[:, x * local_width : (x + 1) * local_width], (block_of(x), c_out)
        )
    shard = lax.psum_scatter(grads, ("tensor", "dp"), scatter_dimension=0, tiled=True).astype(F32)

    grad_mixed = product(out_t, grad_low, CT).astype(BF16)
    grad_one = 0.0
    grad_qkv, sums = [], []
    for head in range(heads):
        parts = []
        for x in range(QUARTERS):
            first = x * local_width + head * HEAD_DIM
            part = grad_mixed[first : first + HEAD_DIM]
            parts.append(swap(part, x) if x else part)
        deltas = attend_backward(
            info, qkv, jnp.concatenate(parts, axis=1), outs[head], lses[head], head
        )
        span = 3 * HEAD_DIM
        parts = []
        for x in range(QUARTERS):
            part = deltas[:, x * QUARTER : (x + 1) * QUARTER]
            parts.append(swap(part, x) if x else part)
        weights = jnp.concatenate([w[:, head * span : (head + 1) * span] for w in qkv_t], axis=1)
        grad_one = grad_one + product(jnp.concatenate(parts, axis=0), weights, CT)
        grad_qkv.append(product(normed, deltas, CT))
        sums.append(jnp.sum(deltas, axis=1, dtype=F32))
    grad_qkv = jnp.concatenate(grad_qkv, axis=1)
    sums = jnp.concatenate(sums)

    unit_one, scale_one = normalise(inputs)
    grad_tokens = (grad_middle + normalise_back(grad_one * gains[0], unit_one, scale_one)).astype(
        BF16
    )

    stats = jnp.stack(
        [
            jnp.sum(grad_two * unit_two, axis=0),
            jnp.sum(grad_two, axis=0),
            jnp.sum(grad_low, axis=0, dtype=F32),
            jnp.sum(grad_result, axis=0),
        ]
        + grad_hidden
    )
    kinds = stats.shape[0]
    stats = stats.reshape(kinds, n_dp, rows).transpose(1, 0, 2).reshape(n_dp, kinds * rows)
    stats = jnp.concatenate([stats, jnp.broadcast_to(sums, (n_dp, qkv_cols))], axis=1)
    length = stats.shape[1]
    stats = jnp.concatenate(pieces(stats), axis=1).astype(BF16)
    stat_rows = -(-3 * length // (16 * qkv_cols)) * 16
    stats = jnp.pad(stats, ((0, 0), (0, stat_rows * qkv_cols - 3 * length)))
    send = jnp.concatenate(
        [
            grad_qkv.astype(BF16).reshape(n_dp, rows, qkv_cols),
            stats.reshape(n_dp, stat_rows, qkv_cols),
        ],
        axis=1,
    )
    received = lax.all_to_all(send, "dp", 0, 0)
    qkv_total = jnp.sum(received[:, :rows], axis=0, dtype=F32)
    stats = jnp.sum(received[:, rows:], axis=0, dtype=F32).reshape(-1)[: 3 * length]
    stats = jnp.sum(stats.reshape(3, length), axis=0)
    sums = stats[kinds * rows :]

    shard_weights = qkv_part.astype(F32)
    shift_one = jnp.sum(shard_weights * sums, axis=1)
    gain_one = (
        jnp.sum(shard_weights * qkv_total, axis=1) - shift_part[0].astype(F32) * shift_one
    ) / gain_part[0].astype(F32)
    stats = jnp.concatenate([stats[: kinds * rows].reshape(kinds, rows), shift_one[None], gain_one[None]])
    stats = stats + swap(stats, 2)
    stats = stats + swap(stats, 1)

    qkv_shard = (
        qkv_total.reshape(rows, heads, 3, HEAD_DIM).transpose(0, 2, 1, 3).reshape(rows, 3, local_width)
    )
    by_part = sums.reshape(heads, 3, HEAD_DIM)
    head_sums = jnp.stack([by_part[:, 0].reshape(-1), by_part[:, 2].reshape(-1)])
    head_shard = lax.dynamic_slice_in_dim(head_sums, lax.axis_index("dp") * few, few, 1)
    hidden_shard = lax.dynamic_index_in_dim(stats[4:8], own, 0, keepdims=False)
    return (
        result,
        grad_tokens,
        qkv_shard,
        shard[:, c_out:].T,
        shard[:, :c_down],
        shard[:, c_down:c_out].T,
        jnp.stack([stats[9], stats[0]]),
        jnp.stack([stats[8], stats[1], stats[2], stats[3]]),
        head_shard,
        hidden_shard,
    )


def solution(mesh):
    placed = (
        P(("dp", "tensor"), None),
        P(("dp", "tensor"), None),
        P(),
        P("dp"),
        P(None, "dp", None, "tensor"),
        P(None, "tensor", "dp"),
        P(None, "dp", "tensor"),
        P(None, "tensor", "dp"),
        P(None, None, "dp"),
        P(None, None, "dp"),
        P(None, None, ("tensor", "dp")),
        P(None, ("tensor", "dp")),
    )
    return jax.shard_map(
        functools.partial(local, mesh.shape["dp"]),
        mesh=mesh,
        in_specs=placed,
        out_specs=(
            P(("dp", "tensor"), None),
            P(("dp", "tensor"), None),
            P("dp", None, "tensor"),
            P("tensor", "dp"),
            P("dp", "tensor"),
            P("tensor", "dp"),
            P(None, "dp"),
            P(None, "dp"),
            P(None, ("tensor", "dp")),
            P(("tensor", "dp")),
        ),
        check_vma=False,
    )
```

time: 2170 us -> 528 us (0.24)
  the two profiles are of different devices: /device:TPU:0 before, /device:TPU:9 now
where the time goes in v1:
time: 528 us; the launch traced here: 524 us
  Pallas kernels  159 us (30%)
  matrix products  99.5 us (19%)
  local copies, waits for them, and re-layouts  72.7 us (14%)
  waiting for transfers between devices  69.4 us (13%)
  other arithmetic  56.8 us (11%)
  starting transfers between devices  49.7 us (9%)
  between operations  17.5 us (3%)
    pallas_call x3, Pallas kernels, attend_backward(): pl.pallas_call(backward_kernel, grid_spec=pltpu.PrefetchScalarGridSpec(nu...  104 us
    dot_general x37, matrix products, product(): return lax.dot_general(left, right, dims, preferred_element_type=F32)  99.5 us
    pallas_call x3, Pallas kernels, attend_forward(): pl.pallas_call(forward_kernel, grid_spec=pltpu.PrefetchScalarGridSpec(num...  54.7 us
    ppermute x32, waiting for transfers between devices, swap(): lax.ppermute(values, 'tensor', [(i, i ^ mask) for i in range(QUARTERS)])  54.4 us
    ppermute x32, starting transfers between devices, swap(): lax.ppermute(values, 'tensor', [(i, i ^ mask) for i in range(QUARTERS)])  36.4 us
    concatenate x1, other arithmetic, local(): jnp.concatenate([jnp.concatenate(grad_up, axis=0), jnp.concatenate(grad_d...  23 us
    unnamed x222, local copies, waits for them, and re-layouts  20 us
    ppermute x7, waiting for transfers between devices, gather_dp(): lax.ppermute(part, 'dp', [((i + k) % count, i) for i in range(count)])  14.9 us
  transfers between devices with their start and end apart: 42, of which 15 were waited for; matrix products, arithmetic and copies ran while one was open for 27% of the time, Pallas kernels for 30%

profile of v1, /device:TPU:9, one launch (start us, length us, event | category | flops | bytes accessed | tf_op | source)
XLA Modules:
  0.0 524.3 jit_solution(10060037419662294241)
XLA Ops:
  17.8 3.3 collective-permute-start.1
  34.2 9.4 %collective-permute-done.2 = bf16[112,576]{1,0:T(8,128)(2,1)} collective-permute-done((bf16[112,576]{1,0:T(8,128)(2,1)}, bf16[112,576]{1,0:T(8,128)(2,1)}, u32[]{:S(2)}, u32[]{:S(2)}) %collective-permute-start.2) | collective-permute-done | bytes 129056 | tf_op jit(solution)/shard_map/ppermute | solution.py:297
  45.8 3.4 collective-permute-done.3
  49.2 3.0 collective-permute-start.7
  71.1 9.0 %collective-permute-done.8 = bf16[1024,768]{0,1:T(8,128)(2,1)S(1)} collective-permute-done((bf16[1024,768]{0,1:T(8,128)(2,1)S(1)}, bf16[1024,768]{0,1:T(8,128)(2,1)S(1)}, u32[]{:S(2)}, u32[]{:S(2)}) %collective-permute-start.8) | collective-permute-done | bytes 1572896 | tf_op jit(solution)/shard_map/ppermute | solution.py:290
  80.2 6.9 %collective-permute-start.9 = (bf16[1024,768]{0,1:T(8,128)(2,1)S(1)}, bf16[1024,768]{0,1:T(8,128)(2,1)S(1)}, u32[]{:S(2)}, u32[]{:S(2)}) collective-permute-start(bf16[1024,768]{0,1:T(8,128)(2,1)S(1)} %collective-permute-done.8), channel_id=1, source_target_pairs={{0,1},{1,0},{2,3},{3,2},{4,5},{5,4},{6,7},{7,6},{8,9},{9,8},{10,11... | collective-permute-start | bytes 4718600 | tf_op jit(solution)/shard_map/ppermute | solution.py:290
  92.2 4.6 fusion.12
  104.2 18.1 %attend_forward.3 = (bf16[64,4096]{1,0:T(8,128)(2,1)}, f32[1,4096]{1,0:T(1,128)}) custom-call(s32[2]{0:T(128)} %pad_add_fusion.info, bf16[3,3,64,4096]{3,2,1,0:T(8,128)(2,1)} %pad_maximum_fusion.1.q_ref.k_ref.v_ref, bf16[3,3,64,4096]{3,2,1,0:T(8,128)(2,1)} %pad_maximum_fusion.1.q_ref.k_ref.v_ref, bf16[3,3,64,4096]{3,2,1,0:T(8,128)(2,1)} %pad_maximum_fusion.1.q_ref.k_ref.v_ref), custom_call_target="tpu_custom_call" | custom-call | flops 17999998976 | bytes 2200000 | tf_op jit(solution)/shard_map/attend_forward/pallas_call | solution.py:130
  123.6 18.5 %attend_forward.4 = (bf16[64,4096]{1,0:T(8,128)(2,1)}, f32[1,4096]{1,0:T(1,128)}) custom-call(s32[2]{0:T(128)} %pad_add_fusion.info, bf16[3,3,64,4096]{3,2,1,0:T(8,128)(2,1)} %pad_maximum_fusion.1.q_ref.k_ref.v_ref, bf16[3,3,64,4096]{3,2,1,0:T(8,128)(2,1)} %pad_maximum_fusion.1.q_ref.k_ref.v_ref, bf16[3,3,64,4096]{3,2,1,0:T(8,128)(2,1)} %pad_maximum_fusion.1.q_ref.k_ref.v_ref), custom_call_target="tpu_custom_call" | custom-call | flops 17999998976 | bytes 2200000 | tf_op jit(solution)/shard_map/attend_forward/pallas_call | solution.py:130
  143.8 18.1 %attend_forward.5 = (bf16[64,4096]{1,0:T(8,128)(2,1)}, f32[1,4096]{1,0:T(1,128)}) custom-call(s32[2]{0:T(128)} %pad_add_fusion.info, bf16[3,3,64,4096]{3,2,1,0:T(8,128)(2,1)} %pad_maximum_fusion.1.q_ref.k_ref.v_ref, bf16[3,3,64,4096]{3,2,1,0:T(8,128)(2,1)} %pad_maximum_fusion.1.q_ref.k_ref.v_ref, bf16[3,3,64,4096]{3,2,1,0:T(8,128)(2,1)} %pad_maximum_fusion.1.q_ref.k_ref.v_ref), custom_call_target="tpu_custom_call" | custom-call | flops 17999998976 | bytes 2200000 | tf_op jit(solution)/shard_map/attend_forward/pallas_call | solution.py:130
  167.8 3.3 collective-permute-start.18
  173.4 4.5 collective-permute-done.16
  178.0 2.8 collective-permute-done.17
  182.5 8.8 %fusion.168 = (bf16[768,192]{1,0:T(8,128)(2,1)}, bf16[768,192]{1,0:T(8,128)(2,1)}, bf16[768,192]{1,0:T(8,128)(2,1)}, bf16[768,192]{1,0:T(8,128)(2,1)}, bf16[768,...) fusion(bf16[3072,2432]{1,0:T(8,128)(2,1)} %all-gather.2.cloned., ...), kind=kLoop, calls=%fused_computation.331 | loop fusion | bytes 9437208 | tf_op jit(solution)/shard_map/slice | solution.py:477
  191.4 3.1 fusion.177
  202.7 4.1 convert_reduce_fusion.10
  208.2 4.1 convert_reduce_fusion.11
  213.8 4.1 convert_reduce_fusion.9
  219.4 5.2 convert_reduce_fusion.8
  224.6 4.7 multiply_reduce_fusion
  233.6 2.5 convolution_convert_fusion.1
  236.1 2.4 convolution_convert_fusion.9
  238.5 2.4 convolution_convert_fusion.8
  241.0 2.4 convolution_convert_fusion.7
  245.8 3.3 fusion.94
  249.2 2.9 fusion.95
  252.1 2.9 fusion.97
  255.0 2.9 fusion.96
  271.8 23.0 %maximum_maximum_fusion = bf16[3072,1728]{1,0:T(8,128)(2,1)} fusion(bf16[768,768]{1,0:T(8,128)(2,1)} %fusion.97, bf16[768,768]{1,0:T(8,128)(2,1)} %fusion.96, bf16[768,768]{1,0:T(8,128)(2,1)} %fusion.95, bf16[768,768]{1,0:T(8,128)(2,1)} %fusion.94, bf16[768,768]{1,0:T(8,128)(2,1)} %convolution_convert_fusion.6, bf16[768,768]{1,0:T(8,128)(2,1)} %convolution_convert_fusion.7, ...), kind=kLoop, calls=%fused_computation | loop fusion | flops 95551488 | bytes 20057472 | tf_op jit(solution)/shard_map/concatenate | solution.py:446
  299.0 3.9 fusion.132
  303.0 3.1 fusion.139
  306.1 3.1 fusion.125
  309.2 4.5 add_convert_fusion
  313.7 2.7 copy.332
  320.1 34.6 %attend_backward.4 = bf16[192,4096]{1,0:T(8,128)(2,1)} custom-call(s32[2]{0:T(128)} %pad_add_fusion.info, bf16[3,3,64,4096]{3,2,1,0:T(8,128)(2,1)} %pad_maximum_fusion.1.q_ref.k_ref.v_ref, bf16[3,3,64,4096]{3,2,1,0:T(8,128)(2,1)} %pad_maximum_fusion.1.q_ref.k_ref.v_ref, bf16[3,3,64,4096]{3,2,1,0:T(8,128)(2,1)} %pad_maximum_fusion.1.q_ref.k_ref.v_ref, ...), custom_call_target="tpu_custom_call" | custom-call | flops 32000000000 | bytes 4500000 | tf_op jit(solution)/shard_map/attend_backward/pallas_call | solution.py:248
  354.8 2.7 fusion.171
  360.2 34.7 %attend_backward.3 = bf16[192,4096]{1,0:T(8,128)(2,1)} custom-call(s32[2]{0:T(128)} %pad_add_fusion.info, bf16[3,3,64,4096]{3,2,1,0:T(8,128)(2,1)} %pad_maximum_fusion.1.q_ref.k_ref.v_ref, bf16[3,3,64,4096]{3,2,1,0:T(8,128)(2,1)} %pad_maximum_fusion.1.q_ref.k_ref.v_ref, bf16[3,3,64,4096]{3,2,1,0:T(8,128)(2,1)} %pad_maximum_fusion.1.q_ref.k_ref.v_ref, ...), custom_call_target="tpu_custom_call" | custom-call | flops 32000000000 | bytes 4500000 | tf_op jit(solution)/shard_map/attend_backward/pallas_call | solution.py:248
  397.4 34.6 %attend_backward.5 = bf16[192,4096]{1,0:T(8,128)(2,1)} custom-call(s32[2]{0:T(128)} %pad_add_fusion.info, bf16[3,3,64,4096]{3,2,1,0:T(8,128)(2,1)} %pad_maximum_fusion.1.q_ref.k_ref.v_ref, bf16[3,3,64,4096]{3,2,1,0:T(8,128)(2,1)} %pad_maximum_fusion.1.q_ref.k_ref.v_ref, bf16[3,3,64,4096]{3,2,1,0:T(8,128)(2,1)} %pad_maximum_fusion.1.q_ref.k_ref.v_ref, ...), custom_call_target="tpu_custom_call" | custom-call | flops 32000000000 | bytes 4500000 | tf_op jit(solution)/shard_map/attend_backward/pallas_call | solution.py:248
  433.9 5.8 %convolution_convert_fusion.12 = bf16[768,192]{0,1:T(8,128)(2,1)} fusion(bf16[192,4096]{1,0:T(8,128)(2,1)S(1)} %copy-done.9, bf16[1024,768]{0,1:T(8,128)(2,1)} %copy-done.25, bf16[1024,768]{0,1:T(8,128)(2,1)} %copy-done.23, bf16[1024,768]{0,1:T(8,128)(2,1)} %copy-done.21, bf16[1024,768]{0,1:T(8,128)(2,1)} %copy-done.19), kind=kOutput, calls=%fused_computation.156 | convolution fusion | flops 1233272832 | bytes 8159232 | tf_op jit(solution)/shard_map/dot_general | solution.py:32
  439.7 2.8 convolution_convert_fusion.11
  442.5 2.8 convolution_convert_fusion.10
  454.2 3.5 all-to-all-start
  460.1 7.9 %collective-permute-done.30 = bf16[192,1024]{1,0:T(8,128)(2,1)} collective-permute-done((bf16[192,1024]{1,0:T(8,128)(2,1)}, bf16[192,1024]{1,0:T(8,128)(2,1)}, u32[]{:S(2)}, u32[]{:S(2)}) %collective-permute-start.30) | collective-permute-done | bytes 393248 | tf_op jit(solution)/shard_map/ppermute | solution.py:290
  469.4 3.2 fusion.72
  474.7 10.0 %collective-permute-done.24 = bf16[192,1024]{1,0:T(8,128)(2,1)} collective-permute-done((bf16[192,1024]{1,0:T(8,128)(2,1)}, bf16[192,1024]{1,0:T(8,128)(2,1)}, u32[]{:S(2)}, u32[]{:S(2)}) %collective-permute-start.24) | collective-permute-done | bytes 393248 | tf_op jit(solution)/shard_map/ppermute | solution.py:290
  484.8 2.8 fusion.64
  487.6 3.8 collective-permute-done.35
  491.4 9.1 %collective-permute-done.36 = bf16[192,1024]{1,0:T(8,128)(2,1)S(1)} collective-permute-done((bf16[192,1024]{1,0:T(8,128)(2,1)}, bf16[192,1024]{1,0:T(8,128)(2,1)S(1)}, u32[]{:S(2)}, u32[]{:S(2)}) %collective-permute-start.36) | collective-permute-done | bytes 393248 | tf_op jit(solution)/shard_map/ppermute | solution.py:290
  (453 shorter events, 147.5 us)
Async XLA Ops:
  7.2 175.3 %all-gather.2.cloned.1.call-start = ((), (), s32[]{:S(2)}) async-start(), calls=%async_computation.2 | async-start | bytes 15409152 | tf_op jit(solution)/shard_map/all_gather | solution.py:377
  13.6 499.5 %reduce-scatter.2.cloned.1.call-start = ((), (), s32[]{:S(2)}) async-start(), calls=%async_computation.3 | async-start | bytes 11354112 | tf_op jit(solution)/shard_map/reduce_scatter | solution.py:458
  16.7 14.5 %collective-permute-start = (bf16[112,576]{1,0:T(8,128)(2,1)}, bf16[112,576]{1,0:T(8,128)(2,1)S(1)}, u32[]{:S(2)}, u32[]{:S(2)}) collective-permute-start(bf16[112,576]{1,0:T(8,128)(2,1)} %pad_maximum_fusion.7), channel_id=1, source_target_pairs={{4,0},{8,4},{12,8},{16,12},{20,16},{24,20},{28,24},{0,28},{5,1},{9... | collective-permute-start | bytes 387080 | tf_op jit(solution)/shard_map/ppermute | solution.py:297
  17.8 14.8 %collective-permute-start.1 = (bf16[112,576]{1,0:T(8,128)(2,1)}, bf16[112,576]{1,0:T(8,128)(2,1)S(1)}, u32[]{:S(2)}, u32[]{:S(2)}) collective-permute-start(bf16[112,576]{1,0:T(8,128)(2,1)} %pad_maximum_fusion.7), channel_id=1, source_target_pairs={{8,0},{12,4},{16,8},{20,12},{24,16},{28,20},{0,24},{4,28},{9,1},{1... | collective-permute-start | bytes 387080 | tf_op jit(solution)/shard_map/ppermute | solution.py:297
  21.2 22.4 %collective-permute-start.2 = (bf16[112,576]{1,0:T(8,128)(2,1)}, bf16[112,576]{1,0:T(8,128)(2,1)}, u32[]{:S(2)}, u32[]{:S(2)}) collective-permute-start(bf16[112,576]{1,0:T(8,128)(2,1)} %pad_maximum_fusion.7), channel_id=1, source_target_pairs={{12,0},{16,4},{20,8},{24,12},{28,16},{0,20},{4,24},{8,28},{13,1},{... | collective-permute-start | bytes 387080 | tf_op jit(solution)/shard_map/ppermute | solution.py:297
  21.2 28.0 %collective-permute-start.3 = (bf16[112,576]{1,0:T(8,128)(2,1)}, bf16[112,576]{1,0:T(8,128)(2,1)}, u32[]{:S(2)}, u32[]{:S(2)}) collective-permute-start(bf16[112,576]{1,0:T(8,128)(2,1)} %pad_maximum_fusion.7), channel_id=1, source_target_pairs={{16,0},{20,4},{24,8},{28,12},{0,16},{4,20},{8,24},{12,28},{17,1},{... | collective-permute-start | bytes 387080 | tf_op jit(solution)/shard_map/ppermute | solution.py:297
  21.2 32.0 %collective-permute-start.4 = (bf16[112,576]{1,0:T(8,128)(2,1)}, bf16[112,576]{1,0:T(8,128)(2,1)}, u32[]{:S(2)}, u32[]{:S(2)}) collective-permute-start(bf16[112,576]{1,0:T(8,128)(2,1)} %pad_maximum_fusion.7), channel_id=1, source_target_pairs={{20,0},{24,4},{28,8},{0,12},{4,16},{8,20},{12,24},{16,28},{21,1},{... | collective-permute-start | bytes 387080 | tf_op jit(solution)/shard_map/ppermute | solution.py:297
  24.4 67.8 %copy-start.2 = (bf16[1024,768]{0,1:T(8,128)(2,1)}, bf16[1024,768]{0,1:T(8,128)(2,1)S(1)}, u32[]{:S(2)}) copy-start(bf16[1024,768]{0,1:T(8,128)(2,1)S(1)} %copy.294) | copy-start | bytes 4718596
  31.3 24.9 %collective-permute-start.5 = (bf16[112,576]{1,0:T(8,128)(2,1)}, bf16[112,576]{1,0:T(8,128)(2,1)S(1)}, u32[]{:S(2)}, u32[]{:S(2)}) collective-permute-start(bf16[112,576]{1,0:T(8,128)(2,1)} %pad_maximum_fusion.7), channel_id=1, source_target_pairs={{24,0},{28,4},{0,8},{4,12},{8,16},{12,20},{16,24},{20,28},{25,1},{... | collective-permute-start | bytes 387080 | tf_op jit(solution)/shard_map/ppermute | solution.py:297
  32.7 23.6 %collective-permute-start.6 = (bf16[112,576]{1,0:T(8,128)(2,1)}, bf16[112,576]{1,0:T(8,128)(2,1)S(1)}, u32[]{:S(2)}, u32[]{:S(2)}) collective-permute-start(bf16[112,576]{1,0:T(8,128)(2,1)} %pad_maximum_fusion.7), channel_id=1, source_target_pairs={{28,0},{0,4},{4,8},{8,12},{12,16},{16,20},{20,24},{24,28},{29,1},{... | collective-permute-start | bytes 387080 | tf_op jit(solution)/shard_map/ppermute | solution.py:297
  43.6 36.6 %collective-permute-start.8 = (bf16[1024,768]{0,1:T(8,128)(2,1)S(1)}, bf16[1024,768]{0,1:T(8,128)(2,1)S(1)}, u32[]{:S(2)}, u32[]{:S(2)}) collective-permute-start(bf16[1024,768]{0,1:T(8,128)(2,1)S(1)} %copy.294), channel_id=1, source_target_pairs={{0,2},{1,3},{2,0},{3,1},{4,6},{5,7},{6,4},{7,5},{8,10},{9,11},{10,... | collective-permute-start | bytes 4718600 | tf_op jit(solution)/shard_map/ppermute | solution.py:290
  49.2 38.1 %collective-permute-start.7 = (bf16[1024,768]{0,1:T(8,128)(2,1)S(1)}, bf16[1024,768]{0,1:T(8,128)(2,1)}, u32[]{:S(2)}, u32[]{:S(2)}) collective-permute-start(bf16[1024,768]{0,1:T(8,128)(2,1)S(1)} %copy.294), channel_id=1, source_target_pairs={{0,1},{1,0},{2,3},{3,2},{4,5},{5,4},{6,7},{7,6},{8,9},{9,8},{10,11... | collective-permute-start | bytes 4718600 | tf_op jit(solution)/shard_map/ppermute | solution.py:290
  80.2 11.3 %collective-permute-start.9 = (bf16[1024,768]{0,1:T(8,128)(2,1)S(1)}, bf16[1024,768]{0,1:T(8,128)(2,1)S(1)}, u32[]{:S(2)}, u32[]{:S(2)}) collective-permute-start(bf16[1024,768]{0,1:T(8,128)(2,1)S(1)} %collective-permute-done.8), channel_id=1, source_target_pairs={{0,1},{1,0},{2,3},{3,2},{4,5},{5,4},{6,7},{7,6},{8,9},{9,8},{10,11... | collective-permute-start | bytes 4718600 | tf_op jit(solution)/shard_map/ppermute | solution.py:290
  123.5 41.1 %collective-permute-start.10 = (bf16[64,1024]{1,0:T(8,128)(2,1)S(1)}, bf16[64,1024]{1,0:T(8,128)(2,1)S(1)}, u32[]{:S(2)}, u32[]{:S(2)}) collective-permute-start(bf16[64,1024]{1,0:T(8,128)(2,1)S(1)} %get-tuple-element.167), channel_id=1, source_target_pairs={{0,1},{1,0},{2,3},{3,2},{4,5},{5,4},{6,7},{7,6},{8,9},{9,8},{10,11... | collective-permute-start | bytes 393224 | tf_op jit(solution)/shard_map/ppermute | solution.py:290
  143.2 22.6 %collective-permute-start.11 = (bf16[64,1024]{1,0:T(8,128)(2,1)S(1)}, bf16[64,1024]{1,0:T(8,128)(2,1)S(1)}, u32[]{:S(2)}, u32[]{:S(2)}) collective-permute-start(bf16[64,1024]{1,0:T(8,128)(2,1)S(1)} %get-tuple-element.163), channel_id=1, source_target_pairs={{0,1},{1,0},{2,3},{3,2},{4,5},{5,4},{6,7},{7,6},{8,9},{9,8},{10,11... | collective-permute-start | bytes 393224 | tf_op jit(solution)/shard_map/ppermute | solution.py:290
  163.0 4.3 collective-permute-start.12
  163.1 4.7 collective-permute-start.13
  164.4 6.7 %collective-permute-start.14 = (bf16[64,1024]{1,0:T(8,128)(2,1)S(1)}, bf16[64,1024]{1,0:T(8,128)(2,1)S(1)}, u32[]{:S(2)}, u32[]{:S(2)}) collective-permute-start(bf16[64,1024]{1,0:T(8,128)(2,1)S(1)} %get-tuple-element.162), channel_id=1, source_target_pairs={{0,2},{1,3},{2,0},{3,1},{4,6},{5,7},{6,4},{7,5},{8,10},{9,11},{10,... | collective-permute-start | bytes 393224 | tf_op jit(solution)/shard_map/ppermute | solution.py:290
  164.6 8.8 %collective-permute-start.15 = (bf16[64,1024]{1,0:T(8,128)(2,1)S(1)}, bf16[64,1024]{1,0:T(8,128)(2,1)S(1)}, u32[]{:S(2)}, u32[]{:S(2)}) collective-permute-start(bf16[64,1024]{1,0:T(8,128)(2,1)S(1)} %get-tuple-element.158), channel_id=1, source_target_pairs={{0,2},{1,3},{2,0},{3,1},{4,6},{5,7},{6,4},{7,5},{8,10},{9,11},{10,... | collective-permute-start | bytes 393224 | tf_op jit(solution)/shard_map/ppermute | solution.py:290
  165.9 12.1 %collective-permute-start.16 = (bf16[64,1024]{1,0:T(8,128)(2,1)S(1)}, bf16[64,1024]{1,0:T(8,128)(2,1)S(1)}, u32[]{:S(2)}, u32[]{:S(2)}) collective-permute-start(bf16[64,1024]{1,0:T(8,128)(2,1)S(1)} %get-tuple-element.165), channel_id=1, source_target_pairs={{0,3},{1,2},{2,1},{3,0},{4,7},{5,6},{6,5},{7,4},{8,11},{9,10},{10,... | collective-permute-start | bytes 393224 | tf_op jit(solution)/shard_map/ppermute | solution.py:290
  167.4 13.4 %collective-permute-start.17 = (bf16[64,1024]{1,0:T(8,128)(2,1)S(1)}, bf16[64,1024]{1,0:T(8,128)(2,1)S(1)}, u32[]{:S(2)}, u32[]{:S(2)}) collective-permute-start(bf16[64,1024]{1,0:T(8,128)(2,1)S(1)} %get-tuple-element.161), channel_id=1, source_target_pairs={{0,3},{1,2},{2,1},{3,0},{4,7},{5,6},{6,5},{7,4},{8,11},{9,10},{10,... | collective-permute-start | bytes 393224 | tf_op jit(solution)/shard_map/ppermute | solution.py:290
  167.8 14.6 %collective-permute-start.18 = (bf16[64,1024]{1,0:T(8,128)(2,1)S(1)}, bf16[64,1024]{1,0:T(8,128)(2,1)S(1)}, u32[]{:S(2)}, u32[]{:S(2)}) collective-permute-start(bf16[64,1024]{1,0:T(8,128)(2,1)S(1)} %get-tuple-element.157), channel_id=1, source_target_pairs={{0,3},{1,2},{2,1},{3,0},{4,7},{5,6},{6,5},{7,4},{8,11},{9,10},{10,... | collective-permute-start | bytes 393224 | tf_op jit(solution)/shard_map/ppermute | solution.py:290
  195.7 50.1 %copy-start.68 = (f32[768]{0:T(1024)}, f32[768]{0:T(1024)S(1)}, u32[]{:S(2)}) copy-start(f32[768]{0:T(1024)S(1)} %get-tuple-element.95) | copy-start | bytes 9220
  195.7 53.4 %copy-start.70 = (f32[768]{0:T(1024)}, f32[768]{0:T(1024)S(1)}, u32[]{:S(2)}) copy-start(f32[768]{0:T(1024)S(1)} %get-tuple-element.94) | copy-start | bytes 9220
  195.7 56.3 %copy-start.64 = (f32[768]{0:T(1024)}, f32[768]{0:T(1024)S(1)}, u32[]{:S(2)}) copy-start(f32[768]{0:T(1024)S(1)} %get-tuple-element.92) | copy-start | bytes 9220
  195.7 59.2 %copy-start.66 = (f32[768]{0:T(1024)}, f32[768]{0:T(1024)S(1)}, u32[]{:S(2)}) copy-start(f32[768]{0:T(1024)S(1)} %get-tuple-element.93) | copy-start | bytes 9220
  258.8 98.9 %collective-permute-start.19 = (bf16[64,1024]{1,0:T(8,128)(2,1)}, bf16[64,1024]{1,0:T(8,128)(2,1)}, u32[]{:S(2)}, u32[]{:S(2)}) collective-permute-start(bf16[64,1024]{1,0:T(8,128)(2,1)} %get-tuple-element.147), channel_id=1, source_target_pairs={{0,1},{1,0},{2,3},{3,2},{4,5},{5,4},{6,7},{7,6},{8,9},{9,8},{10,11... | collective-permute-start | bytes 393224 | tf_op jit(solution)/shard_map/ppermute | solution.py:290
  258.8 99.5 %collective-permute-start.20 = (bf16[64,1024]{1,0:T(8,128)(2,1)}, bf16[64,1024]{1,0:T(8,128)(2,1)}, u32[]{:S(2)}, u32[]{:S(2)}) collective-permute-start(bf16[64,1024]{1,0:T(8,128)(2,1)} %get-tuple-element.146), channel_id=1, source_target_pairs={{0,2},{1,3},{2,0},{3,1},{4,6},{5,7},{6,4},{7,5},{8,10},{9,11},{10,... | collective-permute-start | bytes 393224 | tf_op jit(solution)/shard_map/ppermute | solution.py:290
  260.1 56.3 %collective-permute-start.25 = (bf16[64,1024]{1,0:T(8,128)(2,1)}, bf16[64,1024]{1,0:T(8,128)(2,1)}, u32[]{:S(2)}, u32[]{:S(2)}) collective-permute-start(bf16[64,1024]{1,0:T(8,128)(2,1)} %get-tuple-element.143), channel_id=1, source_target_pairs={{0,1},{1,0},{2,3},{3,2},{4,5},{5,4},{6,7},{7,6},{8,9},{9,8},{10,11... | collective-permute-start | bytes 393224 | tf_op jit(solution)/shard_map/ppermute | solution.py:290
  260.9 55.8 %collective-permute-start.26 = (bf16[64,1024]{1,0:T(8,128)(2,1)}, bf16[64,1024]{1,0:T(8,128)(2,1)}, u32[]{:S(2)}, u32[]{:S(2)}) collective-permute-start(bf16[64,1024]{1,0:T(8,128)(2,1)} %get-tuple-element.142), channel_id=1, source_target_pairs={{0,2},{1,3},{2,0},{3,1},{4,6},{5,7},{6,4},{7,5},{8,10},{9,11},{10,... | collective-permute-start | bytes 393224 | tf_op jit(solution)/shard_map/ppermute | solution.py:290
  261.1 55.8 %collective-permute-start.27 = (bf16[64,1024]{1,0:T(8,128)(2,1)}, bf16[64,1024]{1,0:T(8,128)(2,1)}, u32[]{:S(2)}, u32[]{:S(2)}) collective-permute-start(bf16[64,1024]{1,0:T(8,128)(2,1)} %get-tuple-element.141), channel_id=1, source_target_pairs={{0,3},{1,2},{2,1},{3,0},{4,7},{5,6},{6,5},{7,4},{8,11},{9,10},{10,... | collective-permute-start | bytes 393224 | tf_op jit(solution)/shard_map/ppermute | solution.py:290
  316.4 42.0 %collective-permute-start.21 = (bf16[64,1024]{1,0:T(8,128)(2,1)S(1)}, bf16[64,1024]{1,0:T(8,128)(2,1)S(1)}, u32[]{:S(2)}, u32[]{:S(2)}) collective-permute-start(bf16[64,1024]{1,0:T(8,128)(2,1)S(1)} %copy-done.52), channel_id=1, source_target_pairs={{0,3},{1,2},{2,1},{3,0},{4,7},{5,6},{6,5},{7,4},{8,11},{9,10},{10,... | collective-permute-start | bytes 393224 | tf_op jit(solution)/shard_map/ppermute | solution.py:290
  316.7 79.9 %collective-permute-start.31 = (bf16[64,1024]{1,0:T(8,128)(2,1)S(1)}, bf16[64,1024]{1,0:T(8,128)(2,1)S(1)}, u32[]{:S(2)}, u32[]{:S(2)}) collective-permute-start(bf16[64,1024]{1,0:T(8,128)(2,1)S(1)} %copy-done.51), channel_id=1, source_target_pairs={{0,1},{1,0},{2,3},{3,2},{4,5},{5,4},{6,7},{7,6},{8,9},{9,8},{10,11... | collective-permute-start | bytes 393224 | tf_op jit(solution)/shard_map/ppermute | solution.py:290
  316.9 79.6 %collective-permute-start.32 = (bf16[64,1024]{1,0:T(8,128)(2,1)S(1)}, bf16[64,1024]{1,0:T(8,128)(2,1)S(1)}, u32[]{:S(2)}, u32[]{:S(2)}) collective-permute-start(bf16[64,1024]{1,0:T(8,128)(2,1)S(1)} %copy-done.50), channel_id=1, source_target_pairs={{0,2},{1,3},{2,0},{3,1},{4,6},{5,7},{6,4},{7,5},{8,10},{9,11},{10,... | collective-permute-start | bytes 393224 | tf_op jit(solution)/shard_map/ppermute | solution.py:290
  357.7 38.8 %collective-permute-start.33 = (bf16[64,1024]{1,0:T(8,128)(2,1)S(1)}, bf16[64,1024]{1,0:T(8,128)(2,1)S(1)}, u32[]{:S(2)}, u32[]{:S(2)}) collective-permute-start(bf16[64,1024]{1,0:T(8,128)(2,1)S(1)} %copy-done.49), channel_id=1, source_target_pairs={{0,3},{1,2},{2,1},{3,0},{4,7},{5,6},{6,5},{7,4},{8,11},{9,10},{10,... | collective-permute-start | bytes 393224 | tf_op jit(solution)/shard_map/ppermute | solution.py:290
  358.4 93.6 %collective-permute-start.28 = (bf16[192,1024]{1,0:T(8,128)(2,1)}, bf16[192,1024]{1,0:T(8,128)(2,1)}, u32[]{:S(2)}, u32[]{:S(2)}) collective-permute-start(bf16[192,1024]{1,0:T(8,128)(2,1)} %get-tuple-element.152), channel_id=1, source_target_pairs={{0,1},{1,0},{2,3},{3,2},{4,5},{5,4},{6,7},{7,6},{8,9},{9,8},{10,11... | collective-permute-start | bytes 1179656 | tf_op jit(solution)/shard_map/ppermute | solution.py:290
  397.4 36.4 %copy-start.9 = (bf16[192,4096]{1,0:T(8,128)(2,1)S(1)}, bf16[192,4096]{1,0:T(8,128)(2,1)}, u32[]{:S(2)}) copy-start(bf16[192,4096]{1,0:T(8,128)(2,1)} %attend_backward.3) | copy-start | bytes 4718596
  447.2 10.6 %collective-permute-start.29 = (bf16[192,1024]{1,0:T(8,128)(2,1)}, bf16[192,1024]{1,0:T(8,128)(2,1)}, u32[]{:S(2)}, u32[]{:S(2)}) collective-permute-start(bf16[192,1024]{1,0:T(8,128)(2,1)} %get-tuple-element.151), channel_id=1, source_target_pairs={{0,2},{1,3},{2,0},{3,1},{4,6},{5,7},{6,4},{7,5},{8,10},{9,11},{10,... | collective-permute-start | bytes 1179656 | tf_op jit(solution)/shard_map/ppermute | solution.py:290
  448.6 19.4 %collective-permute-start.30 = (bf16[192,1024]{1,0:T(8,128)(2,1)}, bf16[192,1024]{1,0:T(8,128)(2,1)}, u32[]{:S(2)}, u32[]{:S(2)}) collective-permute-start(bf16[192,1024]{1,0:T(8,128)(2,1)} %get-tuple-element.150), channel_id=1, source_target_pairs={{0,3},{1,2},{2,1},{3,0},{4,7},{5,6},{6,5},{7,4},{8,11},{9,10},{10,... | collective-permute-start | bytes 1179656 | tf_op jit(solution)/shard_map/ppermute | solution.py:290
  449.4 19.9 %collective-permute-start.22 = (bf16[192,1024]{1,0:T(8,128)(2,1)}, bf16[192,1024]{1,0:T(8,128)(2,1)}, u32[]{:S(2)}, u32[]{:S(2)}) collective-permute-start(bf16[192,1024]{1,0:T(8,128)(2,1)} %get-tuple-element.156), channel_id=1, source_target_pairs={{0,1},{1,0},{2,3},{3,2},{4,5},{5,4},{6,7},{7,6},{8,9},{9,8},{10,11... | collective-permute-start | bytes 1179656 | tf_op jit(solution)/shard_map/ppermute | solution.py:290
  449.4 25.2 %collective-permute-start.23 = (bf16[192,1024]{1,0:T(8,128)(2,1)}, bf16[192,1024]{1,0:T(8,128)(2,1)}, u32[]{:S(2)}, u32[]{:S(2)}) collective-permute-start(bf16[192,1024]{1,0:T(8,128)(2,1)} %get-tuple-element.155), channel_id=1, source_target_pairs={{0,2},{1,3},{2,0},{3,1},{4,6},{5,7},{6,4},{7,5},{8,10},{9,11},{10,... | collective-permute-start | bytes 1179656 | tf_op jit(solution)/shard_map/ppermute | solution.py:290
  451.9 32.8 %collective-permute-start.24 = (bf16[192,1024]{1,0:T(8,128)(2,1)}, bf16[192,1024]{1,0:T(8,128)(2,1)}, u32[]{:S(2)}, u32[]{:S(2)}) collective-permute-start(bf16[192,1024]{1,0:T(8,128)(2,1)} %get-tuple-element.154), channel_id=1, source_target_pairs={{0,3},{1,2},{2,1},{3,0},{4,7},{5,6},{6,5},{7,4},{8,11},{9,10},{10,... | collective-permute-start | bytes 1179656 | tf_op jit(solution)/shard_map/ppermute | solution.py:290
  454.2 51.0 %all-to-all-start = ((bf16[8,112,576]{2,1,0:T(8,128)(2,1)}), bf16[8,112,576]{2,1,0:T(8,128)(2,1)S(1)}, u32[]{:S(2)}, u32[]{:S(2)}) async-start(bf16[8,112,576]{2,1,0:T(8,128)(2,1)} %pad_maximum_fusion.3), calls=%async_computation | async-start | bytes 2293760 | tf_op jit(solution)/shard_map/all_to_all | solution.py:512
  457.8 29.8 %collective-permute-start.34 = (bf16[192,1024]{1,0:T(8,128)(2,1)}, bf16[192,1024]{1,0:T(8,128)(2,1)S(1)}, u32[]{:S(2)}, u32[]{:S(2)}) collective-permute-start(bf16[192,1024]{1,0:T(8,128)(2,1)} %get-tuple-element.136), channel_id=1, source_target_pairs={{0,1},{1,0},{2,3},{3,2},{4,5},{5,4},{6,7},{7,6},{8,9},{9,8},{10,11... | collective-permute-start | bytes 1179656 | tf_op jit(solution)/shard_map/ppermute | solution.py:290
  468.0 23.4 %collective-permute-start.35 = (bf16[192,1024]{1,0:T(8,128)(2,1)}, bf16[192,1024]{1,0:T(8,128)(2,1)S(1)}, u32[]{:S(2)}, u32[]{:S(2)}) collective-permute-start(bf16[192,1024]{1,0:T(8,128)(2,1)} %get-tuple-element.135), channel_id=1, source_target_pairs={{0,2},{1,3},{2,0},{3,1},{4,6},{5,7},{6,4},{7,5},{8,10},{9,11},{10,... | collective-permute-start | bytes 1179656 | tf_op jit(solution)/shard_map/ppermute | solution.py:290
  469.3 31.2 %collective-permute-start.36 = (bf16[192,1024]{1,0:T(8,128)(2,1)}, bf16[192,1024]{1,0:T(8,128)(2,1)S(1)}, u32[]{:S(2)}, u32[]{:S(2)}) collective-permute-start(bf16[192,1024]{1,0:T(8,128)(2,1)} %get-tuple-element.134), channel_id=1, source_target_pairs={{0,3},{1,2},{2,1},{3,0},{4,7},{5,6},{6,5},{7,4},{8,11},{9,10},{10,... | collective-permute-start | bytes 1179656 | tf_op jit(solution)/shard_map/ppermute | solution.py:290
  506.1 2.6 collective-permute-start.37
  508.7 2.7 collective-permute-start.38
  (91 other events, 634.9 us)
Sparse Core Ops, SparseCore 0:
  13.7 124.7 all-gather.1
  298.5 141.6 reduce-scatter.1
